TPU v7x, 256 devices: a whole 4x4x8 slice. The times are simulated.
256 devices in a mesh: context: 8 (over y, x_lo), tensor: 8 (over z), fsdp: 4 (over x_hi, core).
Axes of the slice: x: 4 (x_hi: 2, x_lo: 2; x = x_hi * 2 + x_lo), y: 4, z: 8, core: 2. Of those that a mesh axis runs over, the one named last changes fastest.
Arguments:
- queries: bfloat16 [4, 1024, 4096], P('fsdp', 'context', 'tensor'), may hold values from -8 to 8
- keys: bfloat16 [4, 1024, 4096], P('fsdp', 'context', 'tensor'), may hold values from -8 to 8
- values: bfloat16 [4, 1024, 4096], P('fsdp', 'context', 'tensor'), may hold values from -6 to 6
- out_grad: bfloat16 [4, 1024, 4096], P('fsdp', 'context', 'tensor'), may hold values from -6 to 6
- out_weight: bfloat16 [4096, 4096], P('fsdp', 'tensor'), may hold values from -0.09375 to 0.09375
- slopes: float32 [32], P('tensor'), may hold values from 0.00012207031 to 0.05
- counts: int32 [4, 8], P('fsdp', 'context'), may hold values from 1 to 128, 640 in all within a row
- gaps: int32 [4, 1024], P('fsdp', 'context'), may hold values from 1 to 12
Outputs:
- query_grad: bfloat16 [4, 1024, 4096], P('fsdp', 'context', 'tensor')
- key_grad: bfloat16 [4, 1024, 4096], P('fsdp', 'context', 'tensor')
- value_grad: bfloat16 [4, 1024, 4096], P('fsdp', 'context', 'tensor')
- weight_grad: float32 [4096, 4096], P('fsdp', 'tensor')
Inputs may be any that keep to these rules, and one draw needn't show every extreme that they name: In each sequence the counts sum to 640 and the largest is 128.
All inputs are finite; a program needn't handle non-finite values. No bound on the sum of `counts` on one device may be relied on, other than what follows from the above.
Results may differ from a plain program's by a relative error of at most 0.022.
Values may be sent and summed in bfloat16 or wider, within the bound.
A program may use at most 64 MiB of HBM per device.

v0:
```python
import jax
import jax.numpy as jnp
from jax import lax
from jax.sharding import PartitionSpec as P

NEG = -1e30


def laid_out(tiles, dim):
    lengths = list(tiles.shape[1:])
    lengths[dim] *= tiles.shape[0]
    return jnp.moveaxis(tiles, 0, dim).reshape(lengths)


def gather_together(arrays, axis, dims):
    flat = jnp.concatenate([a.reshape(-1) for a in arrays])
    lines, at, finished = (lax.all_gather(flat, axis), 0, [])
    for a, dim in zip(arrays, dims):
        tiles = lines[:, at : at + a.size].reshape(-1, *a.shape)
        finished.append(laid_out(tiles, dim))
        at += a.size
    return tuple(finished)


def copy_for_each(x, axis):
    count = lax.axis_size(axis)
    return lax.all_to_all(jnp.broadcast_to(x[None], (count, *x.shape)), axis, 0, 0, tiled=True)


def collect(x, axis, dim):
    tiles = copy_for_each(x, axis)
    return laid_out(tiles, dim)


def in_one_piece(arrays, axis, dim, along):
    both = jnp.concatenate(arrays, axis=along)
    result, at, finished = (lax.all_gather(both, axis, axis=dim, tiled=True), 0, [])
    for a in arrays:
        finished.append(lax.slice_in_dim(result, at, at + a.shape[along], axis=along))
        at += a.shape[along]
    return tuple(finished)


def per_device(queries, keys, values, out_grad, out_weight, slopes, counts, gaps):
    row_count = queries.shape[1]
    width = queries.shape[2]
    head_count = slopes.shape[0]
    head_size = width // head_count
    scaling = head_size ** (-0.5)
    shard_count = lax.axis_size("context")
    my_start = lax.axis_index("context") * row_count
    total_slots = shard_count * row_count
    all_gaps, all_counts = gather_together((gaps, counts), "context", (1, 1))
    slot_index = jnp.arange(total_slots, dtype=jnp.int32)
    owner = slot_index // row_count
    shard_ids = jnp.arange(shard_count, dtype=jnp.int32)
    slot_limit = jnp.sum(
        jnp.where(owner[:, None] == shard_ids[None, :], all_counts[0][None, :], 0), axis=1
    )
    slot_valid = slot_index % row_count < slot_limit
    offsets = jnp.cumsum(jnp.where(slot_valid, all_gaps[0], 0)).astype(jnp.float32)
    my_valid = lax.dynamic_slice_in_dim(slot_valid, my_start, row_count)
    grad_full = collect(out_grad[0], "tensor", 1)
    grad_masked = jnp.where(my_valid[:, None], grad_full, jnp.zeros_like(grad_full))
    columns = grad_masked
    grad_heads = jnp.dot(
        columns,
        lax.all_gather(out_weight, "fsdp", axis=0, tiled=True),
        preferred_element_type=jnp.float32,
    ).astype(jnp.bfloat16)
    local_q = queries[0]
    local_k = keys[0]
    local_v = values[0]
    key_full, value_full = in_one_piece((local_k, local_v), "context", 0, 1)

    def split(block):
        return block.reshape(block.shape[0], head_count, head_size)

    def scores(q_block, q_start, k_block, k_start):
        query_count = q_block.shape[0]
        key_count = k_block.shape[0]
        logits = (
            jnp.einsum(
                "qhd,khd->hqk", split(q_block), split(k_block), preferred_element_type=jnp.float32
            )
            * scaling
        )
        q_offset = lax.dynamic_slice_in_dim(offsets, q_start, query_count)
        k_offset = lax.dynamic_slice_in_dim(offsets, k_start, key_count)
        k_valid = lax.dynamic_slice_in_dim(slot_valid, k_start, key_count)
        q_slot = q_start + jnp.arange(query_count, dtype=jnp.int32)
        k_slot = k_start + jnp.arange(key_count, dtype=jnp.int32)
        allowed = k_valid[None, :] & (k_slot[None, :] <= q_slot[:, None])
        logits = logits - slopes[:, None, None] * (
            q_offset[None, :, None] - k_offset[None, None, :]
        )
        return (jnp.where(allowed[None], logits, NEG), allowed)

    def visit(needed, work, carry):
        return lax.cond(needed, work, lambda held: held, carry)

    def tile_terms(q_block, g_block, q_lse, q_delta, q_start, k_block, v_block, k_start):
        logits, allowed = scores(q_block, q_start, k_block, k_start)
        probs = jnp.where(allowed[None], jnp.exp(logits - q_lse[:, :, None]), 0.0)
        value_dots = jnp.einsum(
            "qhd,khd->hqk", split(g_block), split(v_block), preferred_element_type=jnp.float32
        )
        dscore = (probs * (value_dots - q_delta[:, :, None])).astype(jnp.bfloat16)
        return (probs.astype(jnp.bfloat16), dscore)

    block = 2 * row_count
    block_total = total_slots // block
    my_last = my_start + row_count - 1

    def mass_step(block_index, carry):
        k_start = block_index * block
        k_block = lax.dynamic_slice_in_dim(key_full, k_start, block, 0)

        def work(state):
            peak, mass = state
            logits, allowed = scores(local_q, my_start, k_block, k_start)
            new_peak = jnp.maximum(peak, jnp.max(logits, axis=2))
            weights = jnp.where(allowed[None], jnp.exp(logits - new_peak[:, :, None]), 0.0)
            return (new_peak, mass * jnp.exp(peak - new_peak) + jnp.sum(weights, axis=2))

        return visit(k_start <= my_last, work, carry)

    start_state = (
        jnp.full((head_count, row_count), NEG, jnp.float32),
        jnp.zeros((head_count, row_count), jnp.float32),
    )
    peak, mass = lax.fori_loop(0, block_total, mass_step, start_state)
    log_total = peak + jnp.log(mass)

    def output_step(block_index, carry):
        k_start = block_index * block
        k_block = lax.dynamic_slice_in_dim(key_full, k_start, block, 0)
        v_block = lax.dynamic_slice_in_dim(value_full, k_start, block, 0)

        def work(acc):
            logits, allowed = scores(local_q, my_start, k_block, k_start)
            probs_b = jnp.where(allowed[None], jnp.exp(logits - log_total[:, :, None]), 0.0).astype(
                jnp.bfloat16
            )
            return acc + jnp.einsum(
                "hqk,khd->qhd", probs_b, split(v_block), preferred_element_type=jnp.float32
            ).reshape(row_count, width)

        return visit(k_start <= my_last, work, carry)

    output_b = lax.fori_loop(
        0, block_total, output_step, jnp.zeros((row_count, width), jnp.float32)
    ).astype(jnp.bfloat16)
    delta = jnp.sum(
        (grad_heads.astype(jnp.float32) * output_b.astype(jnp.float32)).reshape(
            row_count, head_count, head_size
        ),
        axis=2,
    ).T

    def query_step(block_index, carry):
        k_start = block_index * block
        k_block = lax.dynamic_slice_in_dim(key_full, k_start, block, 0)
        v_block = lax.dynamic_slice_in_dim(value_full, k_start, block, 0)

        def work(acc):
            probs_b, dscore = tile_terms(
                local_q, grad_heads, log_total, delta, my_start, k_block, v_block, k_start
            )
            return (
                acc
                + jnp.einsum(
                    "hqk,khd->qhd", dscore, split(k_block), preferred_element_type=jnp.float32
                ).reshape(row_count, width)
                * scaling
            )

        return visit(k_start <= my_last, work, carry)

    query_grad = lax.fori_loop(
        0, block_total, query_step, jnp.zeros((row_count, width), jnp.float32)
    ).astype(jnp.bfloat16)
    stats_lse, stats_delta = in_one_piece((log_total, delta), "context", 1, 0)
    start = jnp.int32(0)
    q_piece, g_piece = in_one_piece((local_q, grad_heads), "context", 0, 1)
    piece_rows = q_piece.shape[0]

    def work(held):
        probs_b, dscore = tile_terms(
            q_piece, g_piece, stats_lse, stats_delta, start, local_k, local_v, my_start
        )
        key_part = (
            jnp.einsum(
                "hqk,qhd->khd", dscore, split(q_piece), preferred_element_type=jnp.float32
            ).reshape(row_count, width)
            * scaling
        )
        value_part = jnp.einsum(
            "hqk,qhd->khd", probs_b, split(g_piece), preferred_element_type=jnp.float32
        ).reshape(row_count, width)
        return jnp.concatenate([key_part, value_part], axis=1)

    key_value_grads = visit(
        start + piece_rows - 1 >= my_start, work, jnp.zeros((row_count, 2 * width), jnp.float32)
    )
    key_grad = key_value_grads[:, :width].astype(jnp.bfloat16)
    value_grad = key_value_grads[:, width:].astype(jnp.bfloat16)
    columns = grad_masked
    weight_share = lax.psum_scatter(
        lax.dot_general(
            columns, output_b, (((0,), (0,)), ((), ())), preferred_element_type=jnp.float32
        ),
        "fsdp",
        scatter_dimension=0,
        tiled=True,
    )
    weight_grad = lax.psum(weight_share, "context")
    return (query_grad[None], key_grad[None], value_grad[None], weight_grad)


def solution(mesh):
    placed = (
        P("fsdp", "context", "tensor"),
        P("fsdp", "context", "tensor"),
        P("fsdp", "context", "tensor"),
        P("fsdp", "context", "tensor"),
        P("fsdp", "tensor"),
        P("tensor"),
        P("fsdp", "context"),
        P("fsdp", "context"),
    )
    return jax.shard_map(
        per_device,
        mesh=mesh,
        in_specs=placed,
        out_specs=(
            P("fsdp", "context", "tensor"),
            P("fsdp", "context", "tensor"),
            P("fsdp", "context", "tensor"),
            P("fsdp", "tensor"),
        ),
        check_vma=False,
    )
```

profile of v0, /device:TPU:2, one launch (start us, length us, event | category | flops | bytes accessed | tf_op | source)
XLA Modules:
  0.0 372.9 jit_solution(449688491105010853)
XLA Ops:
  7.2 1.1 copy.161
  8.3 1.0 copy.162
  9.3 0.7 pad_maximum_fusion.1
  10.1 0.7 all-gather.7.cloned.1.call-update
  10.9 1.1 broadcast_in_dim.191
  11.9 8.5 %all-to-all-start = ((bf16[8,128,512]{2,1,0:T(8,128)(2,1)}), bf16[8,128,512]{2,1,0:T(8,128)(2,1)S(1)}, u32[]{:S(2)}, u32[]{:S(2)}) async-start(bf16[8,128,512]{2,1,0:T(8,128)(2,1)} %broadcast_in_dim.191), calls=%async_computation | async-start | bytes 2097152 | tf_op jit(solution)/shard_map/all_to_all | solution.py:27
  21.1 0.6 dynamic-slice
  22.4 0.1 add_dynamic-update-slice_fusion
  22.5 14.0 %all-reduce = s32[1032]{0:T(1024)S(1)} all-reduce(s32[1032]{0:T(1024)S(1)} %add_dynamic-update-slice_fusion), channel_id=2, replica_groups=mesh['context'=8,'tensor'=8,'fsdp'=4] {'context'}, use_global_device_ids=true, to_apply=%add | all-reduce | flops 1032 | bytes 8256
  36.5 0.1 reshape.459
  36.6 0.1 slice_reduce_fusion.1
  36.7 0.1 select_reduce_fusion.1
  36.8 0.3 reduce-window.9
  37.2 0.1 dynamic_slice.124
  37.3 0.1 slice_reduce_fusion
  37.5 11.6 %all-to-all-done = bf16[8,128,512]{2,1,0:T(8,128)(2,1)S(1)} async-done(((bf16[8,128,512]{2,1,0:T(8,128)(2,1)}), bf16[8,128,512]{2,1,0:T(8,128)(2,1)S(1)}, u32[]{:S(2)}, u32[]{:S(2)}) %all-to-all-start) | async-done | bytes 1048608 | tf_op jit(solution)/shard_map/all_to_all | solution.py:27
  49.1 0.7 copy.163
  49.8 0.1 bitcast_select_fusion
  50.0 16.6 %all-gather.5.cloned.1.call-done = bf16[1024,1024]{0,1:T(8,128)(2,1)} async-done(((bf16[128,1024]{0,1:T(8,128)(2,1)}), bf16[1024,1024]{0,1:T(8,128)(2,1)}) %all-gather.5.cloned.1.call-update) | async-done | bytes 2097168 | tf_op jit(solution)/shard_map/all_gather | solution.py:37
  66.6 2.7 fusion.64
  69.3 1.2 while.47
  69.3 1.0 conditional.8
  69.6 0.1 compare_and_fusion
  69.7 0.1 broadcast_subtract_fusion
  69.9 0.3 fusion.61
  70.2 0.1 select_reduce_fusion
  70.5 3.6 while.48
  70.5 3.5 conditional.9
  70.8 1.0 constant_dynamic-slice_fusion.1
  71.8 0.8 compare_and_fusion.1
  72.6 0.1 broadcast_subtract_fusion.1
  72.7 1.3 fusion.11
  74.2 0.1 copy.164
  74.3 4.5 %fusion.65 = f32[4096,512]{1,0:T(8,128)} fusion(bf16[128,4096]{0,1:T(8,128)(2,1)S(1)} %bitcast_select_fusion, bf16[128,512]{1,0:T(8,128)(2,1)S(1)} %copy.164), kind=kOutput, calls=%fused_computation.117 | convolution fusion | flops 536870912 | bytes 9568256 | tf_op jit(solution)/shard_map/dot_general | solution.py:210
  78.8 31.7 %all-gather.7.cloned.1.call-done = bf16[4096,512]{1,0:T(8,128)(2,1)} async-done(((bf16[1024,512]{1,0:T(8,128)(2,1)}), bf16[4096,512]{1,0:T(8,128)(2,1)}) %all-gather.7.cloned.1.call-update) | async-done | bytes 4194320 | tf_op jit(solution)/shard_map/all_gather | solution.py:68
  110.5 2.9 convert_multiply_fusion
  113.4 0.8 pad_maximum_fusion.2
  114.2 82.0 %reduce-scatter.2.cloned.1.call-done = f32[1024,512]{1,0:T(8,128)} async-done(((f32[4096,512]{1,0:T(8,128)}), f32[1024,512]{1,0:T(8,128)}) %reduce-scatter.2.cloned.1.call-update) | async-done | bytes 2097168 | tf_op jit(solution)/shard_map/reduce_scatter | solution.py:209
  196.3 0.1 reshape.458
  196.4 0.2 reduce_sum.33
  196.7 2.5 while.49
  196.7 2.4 conditional.10
  197.0 1.0 constant_dynamic-slice_fusion.3
  198.0 0.1 compare_and_fusion.2
  198.1 0.1 broadcast_subtract_fusion.2
  198.3 0.3 fusion.32
  198.6 0.4 fusion.35
  199.3 0.8 copy.166
  200.0 36.1 %all_gather.23 = f32[8,1024]{1,0:T(8,128)S(1)} all-gather(f32[8,128]{1,0:T(8,128)S(1)} %pad_maximum_fusion.3), channel_id=1, replica_groups=mesh['context'=8,'tensor'=8,'fsdp'=4] {'context'}, dimensions={1}, use_global_device_ids=true | all-gather | bytes 36864 | tf_op jit(solution)/shard_map/all_gather | solution.py:37
  236.1 15.6 %all-gather.9.cloned.1.call-done = bf16[1024,1024]{1,0:T(8,128)(2,1)} async-done(((bf16[128,1024]{1,0:T(8,128)(2,1)}), bf16[1024,1024]{1,0:T(8,128)(2,1)}) %all-gather.9.cloned.1.call-update) | async-done | bytes 2097168 | tf_op jit(solution)/shard_map/all_gather | solution.py:37
  251.7 10.6 %conditional.4 = (bf16[128,1024]{0,1:T(8,128)(2,1)S(1)}) conditional(s32[]{:T(128)} %convert_element_type.72, () %tuple.110, (s32[]{:T(128)}, pred[1024]{0:T(1024)(128)(4,1)S(1)}, bf16[1024,1024]{1,0:T(8,128)(2,1)}, bf16[1,128,512]{2,1,0:T(8,128)(2,1)S(1)}, f32[4]{0:T(128)S(1)}, /*index=5*/f32[1024]{0:T(1024)S(1)}, f32[8,1024]{1,0:T(8,128)S(1)}, ...), branch_computations={%region_18.19_spmd, %region_19.20_spmd} | conditional | flops 543162496 | bytes 28286098 | solution.py:100
  251.9 0.6 fusion.63
  252.5 0.1 fusion.47
  252.7 1.0 broadcast_subtract_fusion.3
  253.7 2.9 copy.168
  256.6 0.2 fusion.62
  256.8 1.0 copy-done.1
  257.7 1.8 exponential_select_fusion
  259.5 2.3 fusion.43
  261.9 0.4 fusion.44
  262.3 0.1 copy.169
  262.5 0.7 slice_bitcast_fusion
  263.2 100.1 %all-reduce.3.cloned.1.call-done = f32[1024,512]{1,0:T(8,128)} async-done(((f32[1024,512]{1,0:T(8,128)}), f32[1024,512]{1,0:T(8,128)}) %all-reduce.3.cloned.1.call-update) | async-done | bytes 2097168 | tf_op jit(solution)/shard_map/psum | solution.py:217
  363.3 3.1 copy.235
  (85 shorter events, 2.0 us)
Async XLA Ops:
  7.2 3.7 copy-start.5
  7.2 59.4 %all-gather.5.cloned.1.call-start = ((), (), s32[]{:S(2)}) async-start(), calls=%async_computation.2 | async-start | bytes 2359296 | tf_op jit(solution)/shard_map/all_gather | solution.py:37
  10.1 11.0 %copy-start.11 = (u32[256]{0:T(256)S(1)}, u32[256]{0:T(256)}, u32[]{:S(2)}) copy-start(u32[256]{0:T(256)} %constant.260) | copy-start | bytes 3076
  10.1 12.3 %copy-start.8 = (s32[1,128]{1,0:T(1,128)S(1)}, s32[1,128]{1,0:T(1,128)}, u32[]{:S(2)}) copy-start(s32[1,128]{1,0:T(1,128)} %param.29) | copy-start | bytes 1540
  10.1 100.4 %all-gather.7.cloned.1.call-start = ((), (), s32[]{:S(2)}) async-start(), calls=%async_computation.3 | async-start | bytes 5242880 | tf_op jit(solution)/shard_map/all_gather | solution.py:68
  11.9 37.2 %all-to-all-start = ((bf16[8,128,512]{2,1,0:T(8,128)(2,1)}), bf16[8,128,512]{2,1,0:T(8,128)(2,1)S(1)}, u32[]{:S(2)}, u32[]{:S(2)}) async-start(bf16[8,128,512]{2,1,0:T(8,128)(2,1)} %broadcast_in_dim.191), calls=%async_computation | async-start | bytes 2097152 | tf_op jit(solution)/shard_map/all_to_all | solution.py:27
  20.4 175.9 %reduce-scatter.2.cloned.1.call-start = ((), (), s32[]{:S(2)}) async-start(), calls=%async_computation.5 | async-start | bytes 10485760 | tf_op jit(solution)/shard_map/reduce_scatter | solution.py:209
  49.9 19.3 %copy-start = (bf16[1,128,512]{2,1,0:T(8,128)(2,1)S(1)}, bf16[1,128,512]{2,1,0:T(8,128)(2,1)}, u32[]{:S(2)}) copy-start(bf16[1,128,512]{2,1,0:T(8,128)(2,1)} %param.22) | copy-start | bytes 393220
  49.9 19.3 %copy-start.9 = (f32[4]{0:T(128)S(1)}, f32[4]{0:T(128)}, u32[]{:S(2)}) copy-start(f32[4]{0:T(128)} %param.27) | copy-start | bytes 52
  78.8 172.9 %all-gather.9.cloned.1.call-start = ((), (), s32[]{:S(2)}) async-start(), calls=%async_computation.4 | async-start | bytes 2359296 | tf_op jit(solution)/shard_map/all_gather | solution.py:37
  114.2 249.1 %all-reduce.3.cloned.1.call-start = ((), (), s32[]{:S(2)}) async-start(), calls=%async_computation.6 | async-start | bytes 4194304 | tf_op jit(solution)/shard_map/psum | solution.py:217
  196.7 55.0 %copy-start.3 = (bf16[1,128,512]{2,1,0:T(8,128)(2,1)S(1)}, bf16[1,128,512]{2,1,0:T(8,128)(2,1)}, u32[]{:S(2)}) copy-start(bf16[1,128,512]{2,1,0:T(8,128)(2,1)} %param.24) | copy-start | bytes 393220
  196.7 55.0 %copy-start.4 = (bf16[1,128,512]{2,1,0:T(8,128)(2,1)S(1)}, bf16[1,128,512]{2,1,0:T(8,128)(2,1)}, u32[]{:S(2)}) copy-start(bf16[1,128,512]{2,1,0:T(8,128)(2,1)} %param.23) | copy-start | bytes 393220
  251.7 4.8 %copy-start.10 = (f32[4]{0:T(128)}, f32[4]{0:T(128)S(1)}, u32[]{:S(2)}) copy-start(f32[4]{0:T(128)S(1)} %get-tuple-element.954) | copy-start | bytes 52 | tf_op jit(solution)/shard_map/cond
  256.6 1.2 copy-start.2
  256.6 1.2 copy-start.7
  256.8 1.0 copy-start.1
  257.7 1.8 copy-start.6
Sparse Core Ops, SparseCore 0:
  10.2 56.3 all-gather.4
  68.4 42.0 all-gather.6
  113.3 82.8 reduce-scatter.1
  197.9 53.7 all-gather.8
  254.2 109.0 all-reduce.2
where the time goes:
time: 376 us; the launch traced here: 373 us
  waiting for transfers between devices  258 us (69%)
  blocking collectives  50.1 us (13%)
  local copies, waits for them, and re-layouts  20.3 us (5%)
  between operations  15.3 us (4%)
  matrix products  14.3 us (4%)
  starting transfers between devices  8.66 us (2%)
  other arithmetic  5.15 us (1%)
    psum x1, waiting for transfers between devices, per_device(): weight_grad = lax.psum(weight_share, 'context')  100 us
    reduce_scatter x1, waiting for transfers between devices, per_device(): lax.psum_scatter(lax.dot_general(columns, output_b, (((0,), (0,)), ((), (...  82 us
    all_gather x1, blocking collectives, in_one_piece(): lax.all_gather(both, axis, axis=dim, tiled=True)  36.1 us
    all_gather x2, waiting for transfers between devices, in_one_piece(): lax.all_gather(both, axis, axis=dim, tiled=True)  32.2 us
    all_gather x1, waiting for transfers between devices, per_device(): lax.all_gather(out_weight, 'fsdp', axis=0, tiled=True)  31.7 us
    unnamed x1, blocking collectives  14 us
    all_to_all x1, waiting for transfers between devices, copy_for_each(): lax.all_to_all(jnp.broadcast_to(x[None], (count, *x.shape)), axis, 0, 0,...  11.6 us
    all_to_all x1, starting transfers between devices, copy_for_each(): lax.all_to_all(jnp.broadcast_to(x[None], (count, *x.shape)), axis, 0, 0,...  8.47 us
  transfers between devices with their start and end apart: 6, of which 6 were waited for; matrix products, arithmetic and copies ran while one was open for 9% of the time, Pallas kernels for 0%

commit v1 on v0

v1 whole, which is shorter than its diff:
```python
import itertools

import jax
import jax.numpy as jnp
from jax import lax
from jax.experimental import pallas as pl
from jax.experimental.pallas import tpu as pltpu
from jax.sharding import PartitionSpec as P

MESH = pl.DeviceIdType.MESH
F32, BF16 = jnp.float32, jnp.bfloat16
NEG = -1e30
ROWS = 128
HALF = 256


def mm(a, b, ca, cb):
    return lax.dot_general(a, b, (((ca,), (cb,)), ((), ())), preferred_element_type=F32)


def kernel(
    slopes_ref, counts_ref, gaps_ref, q_ref, k_ref, v_ref, g_ref, w_ref,
    dq_ref, dk_ref, dv_ref, wg_ref,
    gap_out, gap_all, k_all, v_all, q_head, g_head, g_all, g_far, w_all,
    prob, o_head, o_out, o_own, o_masked, o_far, hp_own, hp_out, hp_far, hg_out,
    dq_out, dk_acc, dv_acc, dk_out, dv_out,
    part, part_out, half_in, full_in, part2, part2_out, half2_in, full2_in,
    ssem, rsem,
):
    c, z, f = lax.axis_index("context"), lax.axis_index("tensor"), lax.axis_index("fsdp")
    nz = g_all.shape[0]
    y, xl = lax.div(c, 2), lax.rem(c, 2)
    xh, core = lax.div(f, 2), lax.rem(f, 2)
    x = xh * 2 + xl
    place = (x, y)
    side = lax.rem(c + y, 2)
    scaling = ROWS ** (-0.5)
    count = counts_ref[0, 0]
    slope = slopes_ref[0, y]

    def dev(c_=None, z_=None, f_=None):
        return {
            "context": c if c_ is None else c_,
            "tensor": z if z_ is None else z_,
            "fsdp": f if f_ is None else f_,
        }

    def beside(axis, step):
        if axis == 0:
            x2 = lax.rem(x + step + 4, 4)
            return dev(c_=y * 2 + lax.rem(x2, 2), f_=lax.div(x2, 2) * 2 + core)
        return dev(c_=lax.rem(y + step + 4, 4) * 2 + xl)

    right, left = dev(z_=lax.rem(z + 1, nz)), dev(z_=lax.rem(z + nz - 1, nz))
    partner = dev(f_=xh * 2 + 1 - core)
    across = dev(c_=y * 2 + 1 - xl, f_=(1 - xh) * 2 + core)

    send_index, recv_index = itertools.count(), itertools.count()
    sent = []

    def slots(n):
        first = next(recv_index)
        for _ in range(n - 1):
            next(recv_index)
        return first

    def send(src, dst, index, where):
        copy = pltpu.make_async_remote_copy(
            src_ref=src, dst_ref=dst, send_sem=ssem.at[next(send_index)],
            recv_sem=rsem.at[index], device_id=where, device_id_type=MESH,
        )
        copy.start()
        sent.append((None, copy))

    def arrived(dst, index):
        pltpu.make_async_remote_copy(
            src_ref=dst, dst_ref=dst, send_sem=ssem.at[0],
            recv_sem=rsem.at[index], device_id=partner, device_id_type=MESH,
        ).wait_recv()

    def give(mine, src, dst, index, where):
        copy = pltpu.make_async_remote_copy(
            src_ref=src, dst_ref=dst, send_sem=ssem.at[next(send_index)],
            recv_sem=rsem.at[index], device_id=where, device_id_type=MESH,
        )
        pl.when(jnp.logical_not(mine))(copy.start)
        pl.when(mine)(pltpu.make_async_copy(src, dst, rsem.at[index]).start)
        sent.append((mine, copy))

    def taken(mine, dst, index):
        pl.when(jnp.logical_not(mine))(lambda: arrived(dst, index))
        pl.when(mine)(pltpu.make_async_copy(dst, dst, rsem.at[index]).wait)

    def cols(ref, head):
        return ref.at[:, pl.ds(pl.multiple_of(head * ROWS, ROWS), ROWS)]

    def rows(ref, shard):
        return ref.at[pl.ds(pl.multiple_of(shard * ROWS, ROWS), ROWS)]

    lane8 = lax.broadcasted_iota(jnp.int32, (8, ROWS), 1)
    row8 = lax.broadcasted_iota(jnp.int32, (8, ROWS), 0)
    gap_out[...] = jnp.where(
        lane8 < count, jnp.broadcast_to(gaps_ref[...], (8, ROWS)), 0
    ).astype(F32)

    barrier = pltpu.get_barrier_semaphore()
    greeted = [dev(c_=lax.rem(c + d, 8)) for d in range(1, 8)] + [right, left, partner, across]
    for where in greeted:
        pl.semaphore_signal(barrier, inc=1, device_id=where, device_id_type=MESH)
    pl.semaphore_wait(barrier, len(greeted))

    at_gap, at_k, at_v, at_q = slots(8), slots(8), slots(8), slots(4)
    at_ring, at_far, at_w = slots(2 * nz), slots(4), slots(2)
    own_g = pltpu.make_async_copy(g_ref, g_all.at[z], rsem.at[at_ring])
    own_g.start()
    send(g_ref, g_all.at[z], at_ring + 1, right)
    send(g_ref, g_all.at[z], at_ring + nz + 1, left)
    for d in range(8):
        peer = lax.rem(c + d, 8)
        head = lax.div(peer, 2)
        if d == 0:
            gap_all[c] = gap_out[...]
            own_k = pltpu.make_async_copy(cols(k_ref, head), rows(k_all, c), rsem.at[at_k + c])
            own_v = pltpu.make_async_copy(cols(v_ref, head), rows(v_all, c), rsem.at[at_v + c])
            own_k.start()
            own_v.start()
        else:
            send(gap_out, gap_all.at[c], at_gap + c, dev(c_=peer))
            send(cols(k_ref, head), rows(k_all, c), at_k + c, dev(c_=peer))
            send(cols(v_ref, head), rows(v_all, c), at_v + c, dev(c_=peer))
    for d in range(4):
        head = lax.rem(y + d, 4)
        peer = head * 2 + side
        give(peer == c, cols(q_ref, head), q_head.at[y], at_q + y, dev(c_=peer))
    own_w = pltpu.make_async_copy(w_ref, w_all.at[xh], rsem.at[at_w])
    own_w.start()
    send(w_ref, w_all.at[xh], at_w + 1, across)

    to_right, to_left = nz // 2, nz - 1 - nz // 2

    def ring(step):
        if step <= to_right:
            block = g_all.at[lax.rem(z + nz - step, nz)]
            arrived(block, at_ring + step)
            if step < to_right:
                send(block, block, at_ring + step + 1, right)
        if step <= to_left:
            block = g_all.at[lax.rem(z + step, nz)]
            arrived(block, at_ring + nz + step)
            if step < to_left:
                send(block, block, at_ring + nz + step + 1, left)

    ring(1)

    for s in range(8):
        pl.when(s != c)(lambda s=s: arrived(gap_all.at[s], at_gap + s))
    gaps8 = jnp.zeros((8, ROWS), F32)
    before = jnp.zeros((8, ROWS), F32)
    for s in range(8):
        gaps8 = jnp.where(row8 == s, gap_all[s], gaps8)
        before = before + jnp.where(row8 > s, gap_all[s], 0.0)
    r128 = lax.broadcasted_iota(jnp.int32, (ROWS, ROWS), 0)
    l128 = lax.broadcasted_iota(jnp.int32, (ROWS, ROWS), 1)
    upto = (r128 <= l128).astype(BF16)
    offs8 = mm(gaps8.astype(BF16), upto, 1, 0) + jnp.sum(before, axis=1, keepdims=True)
    k_offset = jnp.concatenate([offs8[s : s + 1] for s in range(8)], axis=1)
    k_valid = jnp.concatenate([gaps8[s : s + 1] for s in range(8)], axis=1) > 0.0
    ring(2)
    for s in range(8):
        own = s == c
        taken(own, k_all.at[pl.ds(s * ROWS, ROWS)], at_k + s)
        taken(own, v_all.at[pl.ds(s * ROWS, ROWS)], at_v + s)

    at_o = slots(4)
    shard = [2 * t + lax.rem(xl + t, 2) for t in range(4)]

    def forward(t):
        n = 2 * ROWS * (t + 1)
        ct = shard[t]
        taken(ct == c, q_head.at[t], at_q + t)
        q_gaps = gap_all[ct][0:1]
        q_before = jnp.zeros((1, ROWS), F32)
        for s in range(2 * t + 1):
            q_before = q_before + gap_all[s][0:1] * (s < ct).astype(F32)
        q_offset = jnp.sum(
            jnp.where(l128 <= r128, jnp.broadcast_to(q_gaps, (ROWS, ROWS)), 0.0)
            + jnp.broadcast_to(q_before, (ROWS, ROWS)),
            axis=1, keepdims=True,
        )
        logits = mm(q_head[t], k_all[0:n], 1, 1) * scaling
        logits = logits - slope * (q_offset - k_offset[:, 0:n])
        q_slot = ct * ROWS + lax.broadcasted_iota(jnp.int32, (ROWS, n), 0)
        k_slot = lax.broadcasted_iota(jnp.int32, (ROWS, n), 1)
        allowed = jnp.logical_and(k_valid[:, 0:n], k_slot <= q_slot)
        logits = jnp.where(allowed, logits, NEG)
        peak = jnp.max(logits, axis=1, keepdims=True)
        weight = jnp.where(allowed, jnp.exp(logits - peak), 0.0)
        probs = weight * (1.0 / jnp.sum(weight, axis=1, keepdims=True))
        prob[t, :, 0:n] = probs
        o_head[t] = mm(probs.astype(BF16), v_all[0:n], 1, 0).astype(BF16)
        give(ct == c, o_head.at[t], cols(o_own, y), at_o + y, dev(c_=ct))

    forward(0)
    forward(1)
    ring(3)
    forward(2)
    ring(4)
    forward(3)

    own_g.wait()
    for j in range(4):
        theirs = 4 * (j // 2) + 2 * (1 - core) + j % 2
        send(g_all.at[theirs], g_far.at[j], at_far + j, partner)

    at_of, at_hp = slots(1), slots(1)
    for h in range(4):
        taken(h * 2 + side == c, o_own.at[:, h * ROWS : (h + 1) * ROWS], at_o + h)
    live = lax.broadcasted_iota(jnp.int32, o_own.shape, 0) < count
    o_masked[...] = jnp.where(live, o_own[...], jnp.zeros_like(o_own))
    send(o_masked, o_far, at_of, partner)
    for j in range(4):
        arrived(g_far.at[j], at_far + j)
    arrived(o_far, at_of)

    def both(j):
        mine = g_all[4 * (j // 2) + 2 * core + j % 2]
        return jnp.concatenate([mine, g_far[j]], axis=0)

    outputs = jnp.concatenate([o_masked[...], o_far[...]], axis=0)
    for j in range(4):
        product = mm(both(j), outputs, 0, 0)
        part[0, j] = product[:, 0:HALF]
        for i in range(4):
            part[1, i, j * ROWS : (j + 1) * ROWS] = product[i * ROWS : (i + 1) * ROWS, HALF:]

    class Scatter:
        def __init__(self, axis, terms, out, half, full):
            self.axis, self.terms, self.out, self.half, self.full = axis, terms, out, half, full
            self.at = slots(4)
            self.mid = terms.shape[1] // 2
            p = place[axis]
            self.own = p
            self.far, self.up, self.down = (lax.rem(p + d, 4) for d in (2, 1, 3))

        def start(self):
            self.out[self.far] = self.terms[self.far].astype(BF16)
            far = self.out.at[self.far]
            send(far.at[0 : self.mid], self.half.at[0], self.at, beside(self.axis, 1))
            send(far.at[self.mid :], self.half.at[1], self.at + 1, beside(self.axis, -1))

        def middle(self):
            mid = self.mid
            arrived(self.half.at[0], self.at)
            mine = self.terms.at[self.up]
            self.out[self.up, 0:mid] = (mine[0:mid] + self.half[0].astype(F32)).astype(BF16)
            self.out[self.up, mid:] = mine[mid:].astype(BF16)
            send(self.out.at[self.up], self.full.at[0], self.at + 2, beside(self.axis, 1))
            arrived(self.half.at[1], self.at + 1)
            mine = self.terms.at[self.down]
            self.out[self.down, 0:mid] = mine[0:mid].astype(BF16)
            self.out[self.down, mid:] = (mine[mid:] + self.half[1].astype(F32)).astype(BF16)
            send(self.out.at[self.down], self.full.at[1], self.at + 3, beside(self.axis, -1))

        def finish(self):
            arrived(self.full.at[0], self.at + 2)
            arrived(self.full.at[1], self.at + 3)
            return self.terms[self.own] + self.full[0].astype(F32) + self.full[1].astype(F32)

    first = [Scatter(i, part.at[i], part_out.at[i], half_in.at[i], full_in.at[i]) for i in range(2)]
    for scatter in first:
        scatter.start()

    own_w.wait()
    arrived(w_all.at[1 - xh], at_w + 1)
    width = w_all.shape[2]
    for n in range(0, width, HALF):
        total = jnp.zeros((2 * ROWS, HALF), F32)
        for j in range(4):
            wide = w_all.shape[1] // 2
            w_rows = w_all[j // 2, (j % 2) * wide : (j % 2 + 1) * wide, n : n + HALF]
            total = total + mm(both(j), w_rows, 1, 0)
        hp_own[:, n : n + HALF] = total[0:ROWS]
        hp_out[:, n : n + HALF] = total[ROWS:]
    send(hp_out, hp_far, at_hp, partner)
    for scatter in first:
        scatter.middle()
    arrived(hp_far, at_hp)
    hg_out[...] = jnp.where(live, hp_own[...] + hp_far[...], 0.0).astype(BF16)
    at_g = slots(4)
    for d in range(4):
        head = lax.rem(y + d, 4)
        peer = head * 2 + side
        give(peer == c, cols(hg_out, head), g_head.at[y], at_g + y, dev(c_=peer))

    at_dq, at_dk, at_dv = slots(4), slots(8), slots(8)
    for t in (3, 2, 1, 0):
        n = 2 * ROWS * (t + 1)
        ct = shard[t]
        taken(ct == c, g_head.at[t], at_g + t)
        grad = g_head[t]
        delta = jnp.sum(grad.astype(F32) * o_head[t].astype(F32), axis=1, keepdims=True)
        probs = prob[t, :, 0:n]
        dprob = mm(grad, v_all[0:n], 1, 1)
        dscore = (probs * (dprob - delta)).astype(BF16)
        dq_out[t] = (mm(dscore, k_all[0:n], 1, 0) * scaling).astype(BF16)
        give(ct == c, dq_out.at[t], cols(dq_ref, y), at_dq + y, dev(c_=ct))
        dk_part = mm(dscore, q_head[t], 0, 0)
        dv_part = mm(probs.astype(BF16), grad, 0, 0)
        if t == 3:
            dk_acc[...] = dk_part
            dv_acc[...] = dv_part
        else:
            dk_acc[0:n] += dk_part
            dv_acc[0:n] += dv_part
        for s in (2 * t + 1, 2 * t):
            at = slice(s * ROWS, (s + 1) * ROWS)
            dk_out[at] = (dk_acc[at] * scaling).astype(BF16)
            dv_out[at] = dv_acc[at].astype(BF16)
            there = dev(c_=jnp.int32(s))
            give(s == c, dk_out.at[at], cols(dk_ref.at[xl], y), at_dk + c, there)
            give(s == c, dv_out.at[at], cols(dv_ref.at[xl], y), at_dv + c, there)

    second = [
        Scatter(1 - i, part2.at[i], part2_out.at[i], half2_in.at[i], full2_in.at[i])
        for i in range(2)
    ]
    for i in range(2):
        part2[i] = first[i].finish().reshape(part2.shape[1:])
        second[i].start()
    for i in range(2):
        second[i].middle()
    unit = xl * 4 + y
    for i in range(2):
        wg_ref[unit, :, i * HALF : (i + 1) * HALF] = second[i].finish().astype(BF16)
    at_x, at_y = slots(1), slots(8)
    other = dev(c_=y * 2 + 1 - xl)
    send(wg_ref.at[unit], wg_ref.at[unit], at_x, other)
    send(wg_ref.at[unit], wg_ref.at[unit], at_y, beside(1, 1))
    send(wg_ref.at[unit], wg_ref.at[unit], at_y + 1, beside(1, -1))
    unit2 = (1 - xl) * 4 + y
    arrived(wg_ref.at[unit2], at_x)
    send(wg_ref.at[unit2], wg_ref.at[unit2], at_y + 2, beside(1, 1))
    send(wg_ref.at[unit2], wg_ref.at[unit2], at_y + 3, beside(1, -1))
    below, above, far = (lax.rem(y + d, 4) for d in (3, 1, 2))
    columns = (xl * 4, (1 - xl) * 4)
    mid = ROWS // 2
    for i, column in enumerate(columns):
        low = wg_ref.at[column + below]
        arrived(low, at_y + 2 * i)
        send(low.at[0:mid], low.at[0:mid], at_y + 4 + 2 * i, beside(1, 1))
        high = wg_ref.at[column + above]
        arrived(high, at_y + 2 * i + 1)
        send(high.at[mid:], high.at[mid:], at_y + 5 + 2 * i, beside(1, -1))

    for h in range(4):
        taken(h * 2 + side == c, dq_ref.at[:, h * ROWS : (h + 1) * ROWS], at_dq + h)
    for s in range(8):
        at = slice((s // 2) * ROWS, (s // 2 + 1) * ROWS)
        taken(s == c, dk_ref.at[s % 2, :, at], at_dk + s)
        taken(s == c, dv_ref.at[s % 2, :, at], at_dv + s)
    for i, column in enumerate(columns):
        last = wg_ref.at[column + far]
        arrived(last.at[0:mid], at_y + 4 + 2 * i)
        arrived(last.at[mid:], at_y + 5 + 2 * i)

    for mine, copy in sent:
        if mine is None:
            copy.wait_send()
        else:
            pl.when(jnp.logical_not(mine))(copy.wait_send)
    assert next(send_index) <= ssem.shape[0] and next(recv_index) <= rsem.shape[0]


def per_device(queries, keys, values, out_grad, out_weight, slopes, counts, gaps):
    width = queries.shape[2]
    nz = lax.axis_size("tensor")
    vmem, hbm = pl.BlockSpec(memory_space=pltpu.VMEM), pl.BlockSpec(memory_space=pl.ANY)
    smem = pl.BlockSpec(memory_space=pltpu.SMEM)

    def v(dtype, *shape):
        return pltpu.VMEM(shape, dtype)

    dq, dk, dv, wg = pl.pallas_call(
        kernel,
        out_shape=(
            jax.ShapeDtypeStruct((ROWS, width), BF16),
            jax.ShapeDtypeStruct((2, ROWS, width), BF16),
            jax.ShapeDtypeStruct((2, ROWS, width), BF16),
            jax.ShapeDtypeStruct((8, ROWS, width), BF16),
        ),
        in_specs=[smem, smem, vmem, hbm, hbm, hbm, hbm, hbm],
        out_specs=(vmem, vmem, vmem, vmem),
        scratch_shapes=[
            v(F32, 8, ROWS),
            v(F32, 8, 8, ROWS),
            v(BF16, 8 * ROWS, ROWS),
            v(BF16, 8 * ROWS, ROWS),
            v(BF16, 4, ROWS, ROWS),
            v(BF16, 4, ROWS, ROWS),
            v(BF16, nz, ROWS, width),
            v(BF16, 4, ROWS, width),
            v(BF16, 2, *out_weight.shape),
            v(F32, 4, ROWS, 8 * ROWS),
            v(BF16, 4, ROWS, ROWS),
            v(BF16, 8, ROWS),
            v(BF16, ROWS, width),
            v(BF16, ROWS, width),
            v(BF16, ROWS, width),
            v(F32, ROWS, width),
            v(F32, ROWS, width),
            v(F32, ROWS, width),
            v(BF16, ROWS, width),
            v(BF16, 4, ROWS, ROWS),
            v(F32, 8 * ROWS, ROWS),
            v(F32, 8 * ROWS, ROWS),
            v(BF16, 8 * ROWS, ROWS),
            v(BF16, 8 * ROWS, ROWS),
            v(F32, 2, 4, 4 * ROWS, HALF),
            v(BF16, 2, 4, 4 * ROWS, HALF),
            v(BF16, 2, 2, 2 * ROWS, HALF),
            v(BF16, 2, 2, 4 * ROWS, HALF),
            v(F32, 2, 4, ROWS, HALF),
            v(BF16, 2, 4, ROWS, HALF),
            v(BF16, 2, 2, ROWS // 2, HALF),
            v(BF16, 2, 2, ROWS, HALF),
            pltpu.SemaphoreType.DMA((128,)),
            pltpu.SemaphoreType.DMA((128,)),
        ],
        compiler_params=pltpu.CompilerParams(
            collective_id=0, has_side_effects=True, vmem_limit_bytes=56 << 20
        ),
        name="block_backward",
    )(
        slopes.reshape(1, -1), counts, gaps,
        queries[0], keys[0], values[0], out_grad[0], out_weight,
    )
    dk = (dk[0].astype(F32) + dk[1].astype(F32)).astype(BF16)
    dv = (dv[0].astype(F32) + dv[1].astype(F32)).astype(BF16)
    return dq[None], dk[None], dv[None], wg.reshape(-1, width).astype(F32)


def solution(mesh):
    rows = P("fsdp", "context", "tensor")
    weight = P("fsdp", "tensor")
    placed = (rows, rows, rows, rows, weight, P("tensor"), P("fsdp", "context"))
    return jax.shard_map(
        per_device,
        mesh=mesh,
        in_specs=placed + (P("fsdp", "context"),),
        out_specs=(rows, rows, rows, weight),
        check_vma=False,
    )
```

time: 376 us -> 88.2 us (0.23)
  waiting for transfers between devices: 258 us -> 0 us
  Pallas kernels: 0 us -> 79.8 us
  blocking collectives: 50.1 us -> 0 us
  local copies, waits for them, and re-layouts: 20.3 us -> 0.66 us
  matrix products: 14.3 us -> 0 us
  between operations: 15.3 us -> 1.3 us
  starting transfers between devices: 8.66 us -> 0 us
    psum x1 -> x0, waiting for transfers between devices: 100 us -> none  [per_device(): weight_grad = lax.psum(weight_share, 'context')]
    reduce_scatter x1 -> x0, waiting for transfers between devices: 82 us -> none  [per_device(): lax.psum_scatter(lax.dot_general(columns, output_b, (((0,), (0,)), ((), (...]
    pallas_call x0 -> x1, Pallas kernels: none -> 79.8 us  [per_device(): pl.pallas_call(kernel, out_shape=(jax.ShapeDtypeStruct((ROWS, width), BF1...]
    all_gather x3 -> x0, waiting for transfers between devices: 63.9 us -> none  [the longest x2 32.2 us: in_one_piece(): lax.all_gather(both, axis, axis=dim, tiled=True)]
    all_gather x1 -> x0, blocking collectives: 36.1 us -> none  [in_one_piece(): lax.all_gather(both, axis, axis=dim, tiled=True)]
    dot_general x9 -> x0, matrix products: 14.3 us -> none  [the longest x1 4.46 us: per_device(): lax.dot_general(columns, output_b, (((0,), (0,)), ((), ())), preferred_el...]
    unnamed x1 -> x0, blocking collectives: 14 us -> none
    all_to_all x1 -> x0, waiting for transfers between devices: 11.6 us -> none  [copy_for_each(): lax.all_to_all(jnp.broadcast_to(x[None], (count, *x.shape)), axis, 0, 0,...]
  transfers between devices with their start and end apart: 6 -> 0, of which waited for: 6 -> 0; matrix products, arithmetic and copies ran while one was open for 9% -> 0% of each run, Pallas kernels for 0% -> 0%
where the time goes in v1:
time: 88.2 us; the launch traced here: 86.5 us
  Pallas kernels  79.8 us (90%)
  other arithmetic  4.73 us (5%)
  between operations  1.3 us (1%)
    pallas_call x1, Pallas kernels, per_device(): pl.pallas_call(kernel, out_shape=(jax.ShapeDtypeStruct((ROWS, width), BF1...  79.8 us
    convert_element_type x1, other arithmetic, per_device(): return (dq[None], dk[None], dv[None], wg.reshape(-1, width).astype(F32))  2.83 us
    convert_element_type x1, other arithmetic, per_device(): dv = (dv[0].astype(F32) + dv[1].astype(F32)).astype(BF16)  1.89 us

profile of v1, /device:TPU:2, one launch (start us, length us, event | category | flops | bytes accessed | tf_op | source)
XLA Modules:
  0.0 86.5 jit_solution(4668274484477044850)
XLA Ops:
  1.3 79.8 %block_backward.1 = (bf16[128,512]{1,0:T(8,128)(2,1)}, bf16[2,128,512]{2,1,0:T(8,128)(2,1)}, bf16[2,128,512]{2,1,0:T(8,128)(2,1)}, bf16[8,128,512]{2,1,0:T(8,128)(2,1)}) custom-call(f32[1,4]{1,0:T(1,128)} %bitcast.14, s32[1,1]{1,0:T(1,128)S(6)} %copy.13.counts_ref, s32[1,128]{1,0:T(1,128)} %gaps_ref.1, bf16[128,512]{1,0:T(8,128)(2,1)} %bitcast.9, ...), custom_call_target="tpu_custom_call" | custom-call | tf_op jit(solution)/shard_map/block_backward/pallas_call | solution.py:383
  81.1 0.0 copy-start
  81.1 1.9 %add_convert_fusion = (bf16[1,128,512]{2,1,0:T(8,128)(2,1)}, bf16[1,128,512]{2,1,0:T(8,128)(2,1)}) fusion(bf16[2,128,512]{2,1,0:T(8,128)(2,1)} %get-tuple-element.10, bf16[2,128,512]{2,1,0:T(8,128)(2,1)} %get-tuple-element.9), kind=kLoop, calls=%fused_computation.1 | loop fusion | flops 524288 | bytes 786432 | tf_op jit(solution)/shard_map/convert_element_type | solution.py:438
  83.0 2.8 %bitcast_convert_fusion = f32[1024,512]{1,0:T(8,128)} fusion(bf16[8,128,512]{2,1,0:T(8,128)(2,1)} %get-tuple-element.11), kind=kLoop, calls=%fused_computation | loop fusion | flops 524288 | bytes 3145728 | tf_op jit(solution)/shard_map/convert_element_type | solution.py:439
  85.8 0.0 copy-done
  85.8 0.7 copy.14
Async XLA Ops:
  81.1 4.7 %copy-start = (bf16[128,512]{1,0:T(8,128)(2,1)S(1)}, bf16[128,512]{1,0:T(8,128)(2,1)}, u32[]{:S(2)}) copy-start(bf16[128,512]{1,0:T(8,128)(2,1)} %get-tuple-element.8) | copy-start | bytes 393220

commit v2 on v1

--- a/solution.py
+++ b/solution.py
@@ -22,7 +22,7 @@
     slopes_ref, counts_ref, gaps_ref, q_ref, k_ref, v_ref, g_ref, w_ref,
     dq_ref, dk_ref, dv_ref, wg_ref,
     gap_out, gap_all, k_all, v_all, q_head, g_head, g_all, g_far, w_all,
-    prob, o_head, o_out, o_own, o_masked, o_far, hp_own, hp_out, hp_far, hg_out,
+    prob, o_head, o_own, o_masked, o_far, hp_own, hp_out, hp_far, hg_out,
     dq_out, dk_acc, dv_acc, dk_out, dv_out,
     part, part_out, half_in, full_in, part2, part2_out, half2_in, full2_in,
     ssem, rsem,
@@ -110,47 +110,86 @@
     pl.semaphore_wait(barrier, len(greeted))
 
     at_gap, at_k, at_v, at_q = slots(8), slots(8), slots(8), slots(4)
-    at_ring, at_far, at_w = slots(2 * nz), slots(4), slots(2)
-    own_g = pltpu.make_async_copy(g_ref, g_all.at[z], rsem.at[at_ring])
+    at_ring, at_far, at_w = slots(2 * nz), slots(4), slots(7)
+    part_rows = ROWS // 2
+    hops = nz // 2
+
+    def piece(block, h):
+        return g_all.at[block, h * part_rows : (h + 1) * part_rows]
+
+    def to_partner(block, src):
+        mine = lax.rem(lax.div(block, 2), 2) == core
+        j = 2 * lax.div(block, 4) + lax.rem(block, 2)
+        copy = pltpu.make_async_remote_copy(
+            src_ref=src, dst_ref=g_far.at[j], send_sem=ssem.at[next(send_index)],
+            recv_sem=rsem.at[at_far + j], device_id=partner, device_id_type=MESH,
+        )
+        pl.when(jnp.logical_not(mine))(copy.start)
+        sent.append((mine, copy))
+
+    own_g = pltpu.make_async_copy(g_ref, g_all.at[z], rsem.at[at_ring + 2 * nz - 1])
     own_g.start()
-    send(g_ref, g_all.at[z], at_ring + 1, right)
-    send(g_ref, g_all.at[z], at_ring + nz + 1, left)
+    for h in range(2):
+        src = g_ref.at[h * part_rows : (h + 1) * part_rows]
+        send(src, piece(z, h), at_ring + h, right)
+        send(src, piece(z, h), at_ring + nz + h, left)
+    for d in range(1, 8):
+        send(gap_out, gap_all.at[c], at_gap + c, dev(c_=lax.rem(c + d, 8)))
+    gap_all[c] = gap_out[...]
+    color = lax.rem(xl + y, 2)
+    w_half = w_all.shape[1] // 2
+    cuts = (0, 192, 384, 512)
+    w_next = (beside(1, 1), beside(1, -1), dev(c_=y * 2 + 1 - xl))
+
+    def w_piece(ref, half, i):
+        at = pl.multiple_of(half * w_half + cuts[i], 64)
+        return ref.at[pl.ds(at, cuts[i + 1] - cuts[i])]
+
+    for i in range(3):
+        send(w_piece(w_ref, 1 - color, i), w_piece(w_all.at[xh], 1 - color, i), at_w + i, across)
     for d in range(8):
         peer = lax.rem(c + d, 8)
         head = lax.div(peer, 2)
         if d == 0:
-            gap_all[c] = gap_out[...]
             own_k = pltpu.make_async_copy(cols(k_ref, head), rows(k_all, c), rsem.at[at_k + c])
             own_v = pltpu.make_async_copy(cols(v_ref, head), rows(v_all, c), rsem.at[at_v + c])
             own_k.start()
             own_v.start()
         else:
-            send(gap_out, gap_all.at[c], at_gap + c, dev(c_=peer))
             send(cols(k_ref, head), rows(k_all, c), at_k + c, dev(c_=peer))
             send(cols(v_ref, head), rows(v_all, c), at_v + c, dev(c_=peer))
-    for d in range(4):
-        head = lax.rem(y + d, 4)
-        peer = head * 2 + side
-        give(peer == c, cols(q_ref, head), q_head.at[y], at_q + y, dev(c_=peer))
-    own_w = pltpu.make_async_copy(w_ref, w_all.at[xh], rsem.at[at_w])
+        if d < 4:
+            head = lax.rem(y + d, 4)
+            peer = head * 2 + side
+            give(peer == c, cols(q_ref, head), q_head.at[y], at_q + y, dev(c_=peer))
+    to_partner(z, g_ref)
+    own_w = pltpu.make_async_copy(w_ref, w_all.at[xh], rsem.at[at_w + 6])
     own_w.start()
-    send(w_ref, w_all.at[xh], at_w + 1, across)
-
-    to_right, to_left = nz // 2, nz - 1 - nz // 2
-
-    def ring(step):
-        if step <= to_right:
-            block = g_all.at[lax.rem(z + nz - step, nz)]
-            arrived(block, at_ring + step)
-            if step < to_right:
-                send(block, block, at_ring + step + 1, right)
-        if step <= to_left:
-            block = g_all.at[lax.rem(z + step, nz)]
-            arrived(block, at_ring + nz + step)
-            if step < to_left:
-                send(block, block, at_ring + nz + step + 1, left)
-
-    ring(1)
+
+    last = 2 * (hops - 1)
+
+    def ring(k):
+        d, h = k // 2 + 1, k % 2
+        for way, (where, step, base) in enumerate(
+            ((right, nz - d, at_ring), (left, d, at_ring + nz))
+        ):
+            block = lax.rem(z + step, nz)
+            half = way if k == last else h
+            arrived(piece(block, half), base + k)
+            if d + 1 < hops or (d + 1 == hops and h == way):
+                after = min(k + 2, last)
+                send(piece(block, half), piece(block, half), base + after, where)
+            if h == 1:
+                to_partner(block, g_all.at[block])
+        if k == last:
+            to_partner(lax.rem(z + hops, nz), g_all.at[lax.rem(z + hops, nz)])
+
+    def w_pass(i):
+        theirs = w_piece(w_all.at[1 - xh], color, i)
+        arrived(theirs, at_w + i)
+        send(theirs, theirs, at_w + 3 + i, w_next[i])
+
+    ring(0)
 
     for s in range(8):
         pl.when(s != c)(lambda s=s: arrived(gap_all.at[s], at_gap + s))
@@ -165,11 +204,6 @@
     offs8 = mm(gaps8.astype(BF16), upto, 1, 0) + jnp.sum(before, axis=1, keepdims=True)
     k_offset = jnp.concatenate([offs8[s : s + 1] for s in range(8)], axis=1)
     k_valid = jnp.concatenate([gaps8[s : s + 1] for s in range(8)], axis=1) > 0.0
-    ring(2)
-    for s in range(8):
-        own = s == c
-        taken(own, k_all.at[pl.ds(s * ROWS, ROWS)], at_k + s)
-        taken(own, v_all.at[pl.ds(s * ROWS, ROWS)], at_v + s)
 
     at_o = slots(4)
     shard = [2 * t + lax.rem(xl + t, 2) for t in range(4)]
@@ -177,6 +211,9 @@
     def forward(t):
         n = 2 * ROWS * (t + 1)
         ct = shard[t]
+        for j in (2 * t, 2 * t + 1):
+            taken(j == c, k_all.at[j * ROWS : (j + 1) * ROWS], at_k + j)
+            taken(j == c, v_all.at[j * ROWS : (j + 1) * ROWS], at_v + j)
         taken(ct == c, q_head.at[t], at_q + t)
         q_gaps = gap_all[ct][0:1]
         q_before = jnp.zeros((1, ROWS), F32)
@@ -200,17 +237,19 @@
         o_head[t] = mm(probs.astype(BF16), v_all[0:n], 1, 0).astype(BF16)
         give(ct == c, o_head.at[t], cols(o_own, y), at_o + y, dev(c_=ct))
 
+    ring(1)
+    ring(2)
+    w_pass(0)
+    ring(3)
     forward(0)
+    ring(4)
     forward(1)
-    ring(3)
+    ring(5)
     forward(2)
-    ring(4)
+    w_pass(1)
     forward(3)
-
+    ring(6)
     own_g.wait()
-    for j in range(4):
-        theirs = 4 * (j // 2) + 2 * (1 - core) + j % 2
-        send(g_all.at[theirs], g_far.at[j], at_far + j, partner)
 
     at_of, at_hp = slots(1), slots(1)
     for h in range(4):
@@ -218,20 +257,13 @@
     live = lax.broadcasted_iota(jnp.int32, o_own.shape, 0) < count
     o_masked[...] = jnp.where(live, o_own[...], jnp.zeros_like(o_own))
     send(o_masked, o_far, at_of, partner)
+    w_pass(2)
     for j in range(4):
         arrived(g_far.at[j], at_far + j)
-    arrived(o_far, at_of)
 
     def both(j):
         mine = g_all[4 * (j // 2) + 2 * core + j % 2]
         return jnp.concatenate([mine, g_far[j]], axis=0)
-
-    outputs = jnp.concatenate([o_masked[...], o_far[...]], axis=0)
-    for j in range(4):
-        product = mm(both(j), outputs, 0, 0)
-        part[0, j] = product[:, 0:HALF]
-        for i in range(4):
-            part[1, i, j * ROWS : (j + 1) * ROWS] = product[i * ROWS : (i + 1) * ROWS, HALF:]
 
     class Scatter:
         def __init__(self, axis, terms, out, half, full):
@@ -266,12 +298,9 @@
             arrived(self.full.at[1], self.at + 3)
             return self.terms[self.own] + self.full[0].astype(F32) + self.full[1].astype(F32)
 
-    first = [Scatter(i, part.at[i], part_out.at[i], half_in.at[i], full_in.at[i]) for i in range(2)]
-    for scatter in first:
-        scatter.start()
-
     own_w.wait()
-    arrived(w_all.at[1 - xh], at_w + 1)
+    for i in range(3):
+        arrived(w_piece(w_all.at[1 - xh], 1 - color, i), at_w + 3 + i)
     width = w_all.shape[2]
     for n in range(0, width, HALF):
         total = jnp.zeros((2 * ROWS, HALF), F32)
@@ -282,8 +311,19 @@
         hp_own[:, n : n + HALF] = total[0:ROWS]
         hp_out[:, n : n + HALF] = total[ROWS:]
     send(hp_out, hp_far, at_hp, partner)
+
+    arrived(o_far, at_of)
+    outputs = jnp.concatenate([o_masked[...], o_far[...]], axis=0)
+    for j in range(4):
+        product = mm(both(j), outputs, 0, 0)
+        part[0, j] = product[:, 0:HALF]
+        for i in range(4):
+            part[1, i, j * ROWS : (j + 1) * ROWS] = product[i * ROWS : (i + 1) * ROWS, HALF:]
+
+    first = [Scatter(i, part.at[i], part_out.at[i], half_in.at[i], full_in.at[i]) for i in range(2)]
     for scatter in first:
-        scatter.middle()
+        scatter.start()
+
     arrived(hp_far, at_hp)
     hg_out[...] = jnp.where(live, hp_own[...] + hp_far[...], 0.0).astype(BF16)
     at_g = slots(4)
@@ -292,6 +332,10 @@
         peer = head * 2 + side
         give(peer == c, cols(hg_out, head), g_head.at[y], at_g + y, dev(c_=peer))
 
+    for scatter in first:
+        scatter.middle()
+
+    held = []
     at_dq, at_dk, at_dv = slots(4), slots(8), slots(8)
     for t in (3, 2, 1, 0):
         n = 2 * ROWS * (t + 1)
@@ -303,7 +347,7 @@
         dprob = mm(grad, v_all[0:n], 1, 1)
         dscore = (probs * (dprob - delta)).astype(BF16)
         dq_out[t] = (mm(dscore, k_all[0:n], 1, 0) * scaling).astype(BF16)
-        give(ct == c, dq_out.at[t], cols(dq_ref, y), at_dq + y, dev(c_=ct))
+        held.append((ct, dq_out.at[t], cols(dq_ref, y), at_dq + y))
         dk_part = mm(dscore, q_head[t], 0, 0)
         dv_part = mm(probs.astype(BF16), grad, 0, 0)
         if t == 3:
@@ -316,9 +360,13 @@
             at = slice(s * ROWS, (s + 1) * ROWS)
             dk_out[at] = (dk_acc[at] * scaling).astype(BF16)
             dv_out[at] = dv_acc[at].astype(BF16)
-            there = dev(c_=jnp.int32(s))
-            give(s == c, dk_out.at[at], cols(dk_ref.at[xl], y), at_dk + c, there)
-            give(s == c, dv_out.at[at], cols(dv_ref.at[xl], y), at_dv + c, there)
+            held.append((jnp.int32(s), dk_out.at[at], cols(dk_ref.at[xl], y), at_dk + c))
+            held.append((jnp.int32(s), dv_out.at[at], cols(dv_ref.at[xl], y), at_dv + c))
+
+    def release(n):
+        for _ in range(min(n, len(held))):
+            peer, src, dst, index = held.pop(0)
+            give(peer == c, src, dst, index, dev(c_=peer))
 
     second = [
         Scatter(1 - i, part2.at[i], part2_out.at[i], half2_in.at[i], full2_in.at[i])
@@ -327,8 +375,10 @@
     for i in range(2):
         part2[i] = first[i].finish().reshape(part2.shape[1:])
         second[i].start()
+    release(4)
     for i in range(2):
         second[i].middle()
+    release(6)
     unit = xl * 4 + y
     for i in range(2):
         wg_ref[unit, :, i * HALF : (i + 1) * HALF] = second[i].finish().astype(BF16)
@@ -337,10 +387,12 @@
     send(wg_ref.at[unit], wg_ref.at[unit], at_x, other)
     send(wg_ref.at[unit], wg_ref.at[unit], at_y, beside(1, 1))
     send(wg_ref.at[unit], wg_ref.at[unit], at_y + 1, beside(1, -1))
+    release(4)
     unit2 = (1 - xl) * 4 + y
     arrived(wg_ref.at[unit2], at_x)
     send(wg_ref.at[unit2], wg_ref.at[unit2], at_y + 2, beside(1, 1))
     send(wg_ref.at[unit2], wg_ref.at[unit2], at_y + 3, beside(1, -1))
+    release(4)
     below, above, far = (lax.rem(y + d, 4) for d in (3, 1, 2))
     columns = (xl * 4, (1 - xl) * 4)
     mid = ROWS // 2
@@ -352,6 +404,7 @@
         arrived(high, at_y + 2 * i + 1)
         send(high.at[mid:], high.at[mid:], at_y + 5 + 2 * i, beside(1, -1))
 
+    release(len(held))
     for h in range(4):
         taken(h * 2 + side == c, dq_ref.at[:, h * ROWS : (h + 1) * ROWS], at_dq + h)
     for s in range(8):
@@ -371,10 +424,26 @@
     assert next(send_index) <= ssem.shape[0] and next(recv_index) <= rsem.shape[0]
 
 
+def write_out(dq_ref, dk_ref, dv_ref, wg_ref, dq_o, dk_o, dv_o, wg_o, dk_v, dv_v, wg_v, sem):
+    copies = [pltpu.make_async_copy(dq_ref, dq_o, sem.at[8])]
+    copies[0].start()
+    for u in range(8):
+        at = slice(u * ROWS, (u + 1) * ROWS)
+        wg_v[at] = wg_ref[u].astype(F32)
+        copies.append(pltpu.make_async_copy(wg_v.at[at], wg_o.at[at], sem.at[u]))
+        copies[-1].start()
+    for i, (src, mid, dst) in enumerate(((dk_ref, dk_v, dk_o), (dv_ref, dv_v, dv_o))):
+        mid[...] = (src[0].astype(F32) + src[1].astype(F32)).astype(BF16)
+        copies.append(pltpu.make_async_copy(mid, dst, sem.at[9 + i]))
+        copies[-1].start()
+    for copy in copies:
+        copy.wait()
+
+
 def per_device(queries, keys, values, out_grad, out_weight, slopes, counts, gaps):
     width = queries.shape[2]
     nz = lax.axis_size("tensor")
-    vmem, hbm = pl.BlockSpec(memory_space=pltpu.VMEM), pl.BlockSpec(memory_space=pl.ANY)
+    vmem, hbm = pl.BlockSpec(memory_space=pltpu.VMEM), pl.BlockSpec(memory_space=pltpu.HBM)
     smem = pl.BlockSpec(memory_space=pltpu.SMEM)
 
     def v(dtype, *shape):
@@ -383,10 +452,10 @@
     dq, dk, dv, wg = pl.pallas_call(
         kernel,
         out_shape=(
-            jax.ShapeDtypeStruct((ROWS, width), BF16),
-            jax.ShapeDtypeStruct((2, ROWS, width), BF16),
-            jax.ShapeDtypeStruct((2, ROWS, width), BF16),
-            jax.ShapeDtypeStruct((8, ROWS, width), BF16),
+            v(BF16, ROWS, width),
+            v(BF16, 2, ROWS, width),
+            v(BF16, 2, ROWS, width),
+            v(BF16, 8, ROWS, width),
         ),
         in_specs=[smem, smem, vmem, hbm, hbm, hbm, hbm, hbm],
         out_specs=(vmem, vmem, vmem, vmem),
@@ -402,7 +471,6 @@
             v(BF16, 2, *out_weight.shape),
             v(F32, 4, ROWS, 8 * ROWS),
             v(BF16, 4, ROWS, ROWS),
-            v(BF16, 8, ROWS),
             v(BF16, ROWS, width),
             v(BF16, ROWS, width),
             v(BF16, ROWS, width),
@@ -423,20 +491,37 @@
             v(BF16, 2, 4, ROWS, HALF),
             v(BF16, 2, 2, ROWS // 2, HALF),
             v(BF16, 2, 2, ROWS, HALF),
-            pltpu.SemaphoreType.DMA((128,)),
-            pltpu.SemaphoreType.DMA((128,)),
+            pltpu.SemaphoreType.DMA((144,)),
+            pltpu.SemaphoreType.DMA((144,)),
         ],
         compiler_params=pltpu.CompilerParams(
-            collective_id=0, has_side_effects=True, vmem_limit_bytes=56 << 20
+            collective_id=0, has_side_effects=True, vmem_limit_bytes=62 << 20
         ),
         name="block_backward",
     )(
         slopes.reshape(1, -1), counts, gaps,
         queries[0], keys[0], values[0], out_grad[0], out_weight,
     )
-    dk = (dk[0].astype(F32) + dk[1].astype(F32)).astype(BF16)
-    dv = (dv[0].astype(F32) + dv[1].astype(F32)).astype(BF16)
-    return dq[None], dk[None], dv[None], wg.reshape(-1, width).astype(F32)
+    dq, dk, dv, wg = pl.pallas_call(
+        write_out,
+        out_shape=(
+            jax.ShapeDtypeStruct((ROWS, width), BF16),
+            jax.ShapeDtypeStruct((ROWS, width), BF16),
+            jax.ShapeDtypeStruct((ROWS, width), BF16),
+            jax.ShapeDtypeStruct((8 * ROWS, width), F32),
+        ),
+        in_specs=[vmem] * 4,
+        out_specs=(hbm,) * 4,
+        scratch_shapes=[
+            v(BF16, ROWS, width),
+            v(BF16, ROWS, width),
+            v(F32, 8 * ROWS, width),
+            pltpu.SemaphoreType.DMA((11,)),
+        ],
+        compiler_params=pltpu.CompilerParams(vmem_limit_bytes=12 << 20),
+        name="write_out",
+    )(dq, dk, dv, wg)
+    return dq[None], dk[None], dv[None], wg
 
 
 def solution(mesh):

time: 88.2 us -> 79.6 us (0.902)
  the two profiles are of different devices: /device:TPU:2 before, /device:TPU:4 now
where the time goes in v2:
time: 79.6 us; the launch traced here: 79.5 us
  Pallas kernels  78.2 us (98%)
  between operations  1.29 us (2%)
    pallas_call x1, Pallas kernels, per_device(): pl.pallas_call(kernel, out_shape=(v(BF16, ROWS, width), v(BF16, 2, ROWS,...  76.7 us

profile of v2, /device:TPU:4, one launch (start us, length us, event | category | flops | bytes accessed | tf_op | source)
XLA Modules:
  0.0 79.5 jit_solution(17635814327436016400)
XLA Ops:
  1.3 76.7 %block_backward.1 = (bf16[128,512]{1,0:T(8,128)(2,1)S(1)}, bf16[2,128,512]{2,1,0:T(8,128)(2,1)S(1)}, bf16[2,128,512]{2,1,0:T(8,128)(2,1)S(1)}, bf16[8,128,512]{2,1,0:T(8,128)(2,1)S(1)}) custom-call(f32[1,4]{1,0:T(1,128)} %bitcast.12, s32[1,1]{1,0:T(1,128)S(6)} %copy.12.counts_ref, s32[1,128]{1,0:T(1,128)} %gaps_ref.1, bf16[128,512]{1,0:T(8,128)(2,1)} %bitcast.8, ...), custom_call_target="tpu_custom_call" | custom-call | tf_op jit(solution)/shard_map/block_backward/pallas_call | solution.py:452
  78.0 1.5 %write_out.1 = (bf16[128,512]{1,0:T(8,128)(2,1)}, bf16[128,512]{1,0:T(8,128)(2,1)}, bf16[128,512]{1,0:T(8,128)(2,1)}, f32[1024,512]{1,0:T(8,128)}) custom-call(bf16[128,512]{1,0:T(8,128)(2,1)S(1)} %get-tuple-element.12.dq_ref, bf16[2,128,512]{2,1,0:T(8,128)(2,1)S(1)} %get-tuple-element.13.dk_ref, bf16[2,128,512]{2,1,0:T(8,128)(2,1)S(1)} %get-tuple-element.14.dv_ref, ...), custom_call_target="tpu_custom_call" | custom-call | tf_op jit(solution)/shard_map/write_out/pallas_call | solution.py:505

commit v3 on v2

v3 whole, which is shorter than its diff:
```python
import itertools

import jax
import jax.numpy as jnp
from jax import lax
from jax.experimental import pallas as pl
from jax.experimental.pallas import tpu as pltpu
from jax.sharding import PartitionSpec as P

MESH = pl.DeviceIdType.MESH
F32, BF16 = jnp.float32, jnp.bfloat16
NEG = -1e30
ROWS = 128
HALF = 256


def mm(a, b, ca, cb):
    return lax.dot_general(a, b, (((ca,), (cb,)), ((), ())), preferred_element_type=F32)


def kernel(
    slopes_ref, counts_ref, gaps_ref, q_ref, k_ref, v_ref, g_ref, w_ref,
    dq_ref, dk_ref, dv_ref, wg_ref,
    gap_out, gap_all, k_all, v_all, q_head, g_head, g_all, g_far, w_all,
    prob, o_head, o_own, o_masked, o_far, hp_own, hp_out, hp_far, hg_out,
    dq_out, dk_acc, dv_acc, dk_out, dv_out,
    part, part_out, half_in, full_in, part2, part2_out, half2_in, full2_in,
    sem,
):
    c, z, f = lax.axis_index("context"), lax.axis_index("tensor"), lax.axis_index("fsdp")
    nz = g_all.shape[0]
    y, xl = lax.div(c, 2), lax.rem(c, 2)
    xh, core = lax.div(f, 2), lax.rem(f, 2)
    x = xh * 2 + xl
    place = (x, y)
    side = lax.rem(c + y, 2)
    scaling = ROWS ** (-0.5)
    count = counts_ref[...]
    even = lax.rem(y, 2) == 0

    def dev(c_=None, z_=None, f_=None):
        return {
            "context": c if c_ is None else c_,
            "tensor": z if z_ is None else z_,
            "fsdp": f if f_ is None else f_,
        }

    def beside(axis, step):
        if axis == 0:
            x2 = lax.rem(x + step + 4, 4)
            return dev(c_=y * 2 + lax.rem(x2, 2), f_=lax.div(x2, 2) * 2 + core)
        return dev(c_=lax.rem(y + step + 4, 4) * 2 + xl)

    right, left = dev(z_=lax.rem(z + 1, nz)), dev(z_=lax.rem(z + nz - 1, nz))
    partner = dev(f_=xh * 2 + 1 - core)
    across = dev(c_=y * 2 + 1 - xl, f_=(1 - xh) * 2 + core)

    semaphores = itertools.count()
    finals = []

    def slots(n):
        first = next(semaphores)
        for _ in range(n - 1):
            next(semaphores)
        return first

    def send(src, dst, index, where, group, mine=None):
        copy = pltpu.make_async_remote_copy(
            src_ref=src, dst_ref=dst, send_sem=sem.at[group],
            recv_sem=sem.at[index], device_id=where, device_id_type=MESH,
        )
        if mine is None:
            copy.start()
        else:
            pl.when(jnp.logical_not(mine))(copy.start)

    def give(mine, src, dst, index, where, group):
        send(src, dst, index, where, group, mine)
        pl.when(mine)(pltpu.make_async_copy(src, dst, sem.at[index]).start)

    def arrived(dst, index):
        pltpu.make_async_remote_copy(
            src_ref=dst, dst_ref=dst, send_sem=sem.at[index],
            recv_sem=sem.at[index], device_id=partner, device_id_type=MESH,
        ).wait_recv()

    def at_end(group, ref, when=None):
        finals.append((group, ref, when))

    def cols(ref, head):
        return ref.at[:, pl.ds(pl.multiple_of(head * ROWS, ROWS), ROWS)]

    def rows(ref, shard):
        return ref.at[pl.ds(pl.multiple_of(shard * ROWS, ROWS), ROWS)]

    lane8 = lax.broadcasted_iota(jnp.int32, (8, ROWS), 1)
    row8 = lax.broadcasted_iota(jnp.int32, (8, ROWS), 0)
    gap_out[...] = jnp.where(
        lane8 < jnp.broadcast_to(count, (8, ROWS)), jnp.broadcast_to(gaps_ref[...], (8, ROWS)), 0
    ).astype(F32)
    heads = lax.broadcasted_iota(jnp.int32, slopes_ref.shape, 1)
    slope = jnp.sum(jnp.where(heads == y, slopes_ref[...], 0.0), axis=1, keepdims=True)

    barrier = pltpu.get_barrier_semaphore()
    greeted = [dev(c_=lax.rem(c + d, 8)) for d in range(1, 8)] + [right, left, partner, across]
    for where in greeted:
        pl.semaphore_signal(barrier, inc=1, device_id=where, device_id_type=MESH)
    pl.semaphore_wait(barrier, len(greeted))

    at_gap, at_kvq, at_ring, at_far, at_w = slots(1), slots(4), slots(2 * nz), slots(1), slots(7)
    by_gap, by_kv, by_q, by_right, by_left, by_far, by_w = (slots(1) for _ in range(7))
    part_rows = ROWS // 2
    hops = nz // 2

    def piece(block, h):
        return g_all.at[block, h * part_rows : (h + 1) * part_rows]

    def to_partner(block, src):
        mine = lax.rem(lax.div(block, 2), 2) == core
        j = 2 * lax.div(block, 4) + lax.rem(block, 2)
        send(src, g_far.at[j], at_far, partner, by_far, mine)

    own_g = pltpu.make_async_copy(g_ref, g_all.at[z], sem.at[at_ring + 2 * nz - 1])
    own_g.start()
    for h in range(2):
        src = g_ref.at[h * part_rows : (h + 1) * part_rows]
        send(src, piece(z, h), at_ring + h, right, by_right)
        send(src, piece(z, h), at_ring + nz + h, left, by_left)
    pltpu.make_async_copy(gap_out, gap_all.at[c], sem.at[at_gap]).start()
    for d in range(1, 8):
        send(gap_out, gap_all.at[c], at_gap, dev(c_=lax.rem(c + d, 8)), by_gap)
    color = lax.rem(xl + y, 2)
    w_half = w_all.shape[1] // 2
    cuts = (0, 192, 384, 512)
    w_next = (beside(1, 1), beside(1, -1), dev(c_=y * 2 + 1 - xl))

    def w_piece(ref, half, i):
        at = pl.multiple_of(half * w_half + cuts[i], 64)
        return ref.at[pl.ds(at, cuts[i + 1] - cuts[i])]

    for i in range(3):
        there = w_piece(w_all.at[xh], 1 - color, i)
        send(w_piece(w_ref, 1 - color, i), there, at_w + i, across, by_w)
    for d in range(8):
        peer = lax.rem(c + d, 8)
        head = lax.div(peer, 2)
        for src, dst in ((k_ref, k_all), (v_ref, v_all)):
            if d == 0:
                pltpu.make_async_copy(cols(src, head), rows(dst, c), sem.at[at_kvq + y]).start()
            else:
                send(cols(src, head), rows(dst, c), at_kvq + y, dev(c_=peer), by_kv)
        if d < 4:
            head = lax.rem(y + d, 4)
            peer = head * 2 + side
            give(peer == c, cols(q_ref, head), q_head.at[y], at_kvq + y, dev(c_=peer), by_q)
    to_partner(z, g_ref)
    own_w = pltpu.make_async_copy(w_ref, w_all.at[xh], sem.at[at_w + 6])
    own_w.start()
    at_end(by_gap, gap_all.at[0:7])
    at_end(by_kv, w_all.at[0, 0:448])
    for by in (by_right, by_left):
        at_end(by, w_all.at[0, 0 : part_rows * (2 * hops - 1)])
    at_end(by_far, g_far)
    at_end(by_w, w_all.at[0])

    def at_end_heads(by):
        at_end(by, o_head.at[0:3], even)
        at_end(by, o_head, jnp.logical_not(even))

    at_end_heads(by_q)

    last = 2 * (hops - 1)

    def ring(k):
        d, h = k // 2 + 1, k % 2
        for way, (where, step, base) in enumerate(
            ((right, nz - d, at_ring), (left, d, at_ring + nz))
        ):
            block = lax.rem(z + step, nz)
            half = way if k == last else h
            arrived(piece(block, half), base + k)
            if d + 1 < hops or (d + 1 == hops and h == way):
                after = min(k + 2, last)
                by = (by_right, by_left)[way]
                send(piece(block, half), piece(block, half), base + after, where, by)
            if h == 1:
                to_partner(block, g_all.at[block])
        if k == last:
            to_partner(lax.rem(z + hops, nz), g_all.at[lax.rem(z + hops, nz)])

    def w_pass(i):
        theirs = w_piece(w_all.at[1 - xh], color, i)
        arrived(theirs, at_w + i)
        send(theirs, theirs, at_w + 3 + i, w_next[i], by_w)

    ring(0)

    arrived(gap_all, at_gap)
    gaps8 = jnp.zeros((8, ROWS), F32)
    before = jnp.zeros((8, ROWS), F32)
    for s in range(8):
        gaps8 = jnp.where(row8 == s, gap_all[s], gaps8)
        before = before + jnp.where(row8 > s, gap_all[s], 0.0)
    r128 = lax.broadcasted_iota(jnp.int32, (ROWS, ROWS), 0)
    l128 = lax.broadcasted_iota(jnp.int32, (ROWS, ROWS), 1)
    upto = (r128 <= l128).astype(BF16)
    offs8 = mm(gaps8.astype(BF16), upto, 1, 0) + jnp.sum(before, axis=1, keepdims=True)
    k_offset = jnp.concatenate([offs8[s : s + 1] for s in range(8)], axis=1)
    k_valid = jnp.concatenate([gaps8[s : s + 1] for s in range(8)], axis=1) > 0.0

    at_o, by_o = slots(1), slots(1)
    at_end_heads(by_o)
    shard = [2 * t + lax.rem(xl + t, 2) for t in range(4)]

    def forward(t):
        n = 2 * ROWS * (t + 1)
        ct = shard[t]
        arrived(k_all.at[0 : 5 * ROWS], at_kvq + t)
        q_gaps = gap_all[ct][0:1]
        q_before = jnp.zeros((1, ROWS), F32)
        for s in range(2 * t + 1):
            q_before = q_before + gap_all[s][0:1] * (s < ct).astype(F32)
        q_offset = jnp.sum(
            jnp.where(l128 <= r128, jnp.broadcast_to(q_gaps, (ROWS, ROWS)), 0.0)
            + jnp.broadcast_to(q_before, (ROWS, ROWS)),
            axis=1, keepdims=True,
        )
        logits = mm(q_head[t], k_all[0:n], 1, 1) * scaling
        logits = logits - slope * (q_offset - k_offset[:, 0:n])
        q_slot = ct * ROWS + lax.broadcasted_iota(jnp.int32, (ROWS, n), 0)
        k_slot = lax.broadcasted_iota(jnp.int32, (ROWS, n), 1)
        allowed = jnp.logical_and(k_valid[:, 0:n], k_slot <= q_slot)
        logits = jnp.where(allowed, logits, NEG)
        peak = jnp.max(logits, axis=1, keepdims=True)
        weight = jnp.where(allowed, jnp.exp(logits - peak), 0.0)
        probs = weight * (1.0 / jnp.sum(weight, axis=1, keepdims=True))
        prob[t, :, 0:n] = probs
        o_head[t] = mm(probs.astype(BF16), v_all[0:n], 1, 0).astype(BF16)
        give(ct == c, o_head.at[t], cols(o_own, y), at_o, dev(c_=ct), by_o)

    ring(1)
    w_pass(0)
    ring(2)
    ring(3)
    ring(4)
    w_pass(1)
    ring(5)
    forward(0)
    forward(1)
    ring(6)
    w_pass(2)
    forward(2)
    forward(3)
    own_g.wait()

    at_of, at_hp, by_of, by_hp = (slots(1) for _ in range(4))
    arrived(o_own, at_o)
    live = lax.broadcasted_iota(jnp.int32, o_own.shape, 0) < jnp.broadcast_to(count, o_own.shape)
    o_masked[...] = jnp.where(live, o_own[...], jnp.zeros_like(o_own))
    send(o_masked, o_far, at_of, partner, by_of)
    at_end(by_of, o_masked)
    arrived(g_far, at_far)

    def both(j):
        mine = g_all[4 * (j // 2) + 2 * core + j % 2]
        return jnp.concatenate([mine, g_far[j]], axis=0)

    class Scatter:
        def __init__(self, axis, terms, out, half, full, by):
            self.axis, self.terms, self.out, self.half, self.full = axis, terms, out, half, full
            self.at, self.by = slots(6), by
            mid = terms.shape[1] // 2
            self.low, self.high = slice(0, mid), slice(mid, 2 * mid)
            p = place[axis]
            self.own = p
            self.far, self.up, self.down = (lax.rem(p + d, 4) for d in (2, 1, 3))
            self.after, self.behind = beside(axis, 1), beside(axis, -1)

        def pass_on(self, group, at, way, more=None):
            terms = self.terms[group, at]
            if more is not None:
                terms = terms + more.astype(F32)
            self.out[group, at] = terms.astype(BF16)
            index = self.at + 2 + 2 * way + (more is not None)
            where = (self.after, self.behind)[way]
            send(self.out.at[group, at], self.full.at[way, at], index, where, self.by)

        def start(self):
            self.out[self.far] = self.terms[self.far].astype(BF16)
            far = self.out.at[self.far]
            send(far.at[self.low], self.half.at[0], self.at, self.after, self.by)
            send(far.at[self.high], self.half.at[1], self.at + 1, self.behind, self.by)

        def more(self):
            self.pass_on(self.up, self.high, 0)
            self.pass_on(self.down, self.low, 1)

        def middle(self):
            arrived(self.half.at[0], self.at)
            self.pass_on(self.up, self.low, 0, self.half[0])
            arrived(self.half.at[1], self.at + 1)
            self.pass_on(self.down, self.high, 1, self.half[1])

        def finish(self):
            for way in range(2):
                arrived(self.full.at[way, self.low], self.at + 2 + 2 * way)
                arrived(self.full.at[way, self.high], self.at + 3 + 2 * way)
            return self.terms[self.own] + self.full[0].astype(F32) + self.full[1].astype(F32)

    own_w.wait()
    for i in range(3):
        arrived(w_piece(w_all.at[1 - xh], 1 - color, i), at_w + 3 + i)
    width = w_all.shape[2]
    for n in range(0, width, HALF):
        total = jnp.zeros((2 * ROWS, HALF), F32)
        for j in range(4):
            wide = w_all.shape[1] // 2
            w_rows = w_all[j // 2, (j % 2) * wide : (j % 2 + 1) * wide, n : n + HALF]
            total = total + mm(both(j), w_rows, 1, 0)
        hp_own[:, n : n + HALF] = total[0:ROWS]
        hp_out[:, n : n + HALF] = total[ROWS:]
    send(hp_out, hp_far, at_hp, partner, by_hp)
    at_end(by_hp, hp_out)

    arrived(o_far, at_of)
    outputs = jnp.concatenate([o_masked[...], o_far[...]], axis=0)
    for j in range(4):
        product = mm(both(j), outputs, 0, 0)
        part[0, j] = product[:, 0:HALF]
        for i in range(4):
            part[1, i, j * ROWS : (j + 1) * ROWS] = product[i * ROWS : (i + 1) * ROWS, HALF:]

    by_first, by_second = slots(2), slots(1)
    for i in range(2):
        at_end(by_first + i, part_out.at[i, 0:3])
    at_end(by_second, part2_out.at[:, 0:3])
    first = [
        Scatter(i, part.at[i], part_out.at[i], half_in.at[i], full_in.at[i], by_first + i)
        for i in range(2)
    ]
    for scatter in first:
        scatter.start()

    arrived(hp_far, at_hp)
    hg_out[...] = jnp.where(live, hp_own[...] + hp_far[...], 0.0).astype(BF16)
    at_g, by_g = slots(1), slots(1)
    at_end_heads(by_g)
    for d in range(4):
        head = lax.rem(y + d, 4)
        peer = head * 2 + side
        give(peer == c, cols(hg_out, head), g_head.at[y], at_g, dev(c_=peer), by_g)

    for scatter in first:
        scatter.more()
    for scatter in first:
        scatter.middle()

    held = []
    at_dq, at_dk, at_dv, by_dq, by_dkv = (slots(1) for _ in range(5))
    at_end_heads(by_dq)
    at_end(by_dkv, w_all.at[0, 0:448])
    arrived(g_head, at_g)
    for t in (3, 2, 1, 0):
        n = 2 * ROWS * (t + 1)
        ct = shard[t]
        grad = g_head[t]
        delta = jnp.sum(grad.astype(F32) * o_head[t].astype(F32), axis=1, keepdims=True)
        probs = prob[t, :, 0:n]
        dprob = mm(grad, v_all[0:n], 1, 1)
        dscore = (probs * (dprob - delta)).astype(BF16)
        dq_out[t] = (mm(dscore, k_all[0:n], 1, 0) * scaling).astype(BF16)
        dk_part = mm(dscore, q_head[t], 0, 0)
        dv_part = mm(probs.astype(BF16), grad, 0, 0)
        if t == 3:
            dk_acc[...] = dk_part
            dv_acc[...] = dv_part
        else:
            dk_acc[0:n] += dk_part
            dv_acc[0:n] += dv_part
        for s in (2 * t + 1, 2 * t):
            at = slice(s * ROWS, (s + 1) * ROWS)
            dk_out[at] = (dk_acc[at] * scaling).astype(BF16)
            dv_out[at] = dv_acc[at].astype(BF16)

    for d in range(4):
        t = lax.rem(y + d, 4)
        held.append((2 * t + lax.rem(xl + t, 2), dq_out.at[t], cols(dq_ref, y), at_dq, by_dq))
    for d in range(8):
        s = lax.rem(c + d, 8)
        held.append((s, rows(dk_out, s), cols(dk_ref.at[xl], y), at_dk, by_dkv))
        held.append((s, rows(dv_out, s), cols(dv_ref.at[xl], y), at_dv, by_dkv))

    def release(n):
        for _ in range(min(n, len(held))):
            peer, src, dst, index, by = held.pop(0)
            give(peer == c, src, dst, index, dev(c_=peer), by)

    release(6)
    second = [
        Scatter(1 - i, part2.at[i], part2_out.at[i], half2_in.at[i], full2_in.at[i], by_second)
        for i in range(2)
    ]
    for i in range(2):
        part2[i] = first[i].finish().reshape(part2.shape[1:])
        second[i].start()
        second[i].more()
    release(5)
    for i in range(2):
        second[i].middle()
    release(4)
    at_x, at_y, by_all = slots(2), slots(16), slots(1)
    at_end(by_all, wg_ref.at[0:7])
    near, back = beside(1, 1), beside(1, -1)
    other = dev(c_=y * 2 + 1 - xl)
    below, above, far = (lax.rem(y + d, 4) for d in (3, 1, 2))
    columns = (xl * 4, (1 - xl) * 4)
    mid = ROWS // 2

    def unit(column, place_y, i):
        return wg_ref.at[column + place_y, :, i * HALF : (i + 1) * HALF]

    for i in range(2):
        mine = unit(columns[0], y, i)
        mine[...] = second[i].finish().astype(BF16)
        send(mine, mine, at_x + i, other, by_all)
        send(mine, mine, at_y + 2 * i, near, by_all)
        send(mine, mine, at_y + 2 * i + 1, back, by_all)
    release(3)
    for i in range(2):
        mine = unit(columns[1], y, i)
        arrived(mine, at_x + i)
        send(mine, mine, at_y + 4 + 2 * i, near, by_all)
        send(mine, mine, at_y + 4 + 2 * i + 1, back, by_all)
    release(len(held))
    for j, column in enumerate(columns):
        for i in range(2):
            low = unit(column, below, i)
            arrived(low, at_y + 4 * j + 2 * i)
            send(low.at[0:mid], low.at[0:mid], at_y + 8 + 4 * j + 2 * i, near, by_all)
            high = unit(column, above, i)
            arrived(high, at_y + 4 * j + 2 * i + 1)
            send(high.at[mid:], high.at[mid:], at_y + 9 + 4 * j + 2 * i, back, by_all)

    arrived(dq_ref, at_dq)
    arrived(dk_ref, at_dk)
    arrived(dv_ref, at_dv)
    for j, column in enumerate(columns):
        for i in range(2):
            end = unit(column, far, i)
            arrived(end.at[0:mid], at_y + 8 + 4 * j + 2 * i)
            arrived(end.at[mid:], at_y + 9 + 4 * j + 2 * i)

    for group, ref, when in finals:
        wait = pltpu.make_async_remote_copy(
            src_ref=ref, dst_ref=ref, send_sem=sem.at[group],
            recv_sem=sem.at[group], device_id=partner, device_id_type=MESH,
        ).wait_send
        if when is None:
            wait()
        else:
            pl.when(when)(wait)
    assert next(semaphores) == sem.shape[0], next(semaphores)


def write_out(dq_ref, dk_ref, dv_ref, wg_ref, dq_o, dk_o, dv_o, wg_o, dk_v, dv_v, wg_v, sem):
    copies = [pltpu.make_async_copy(dq_ref, dq_o, sem.at[8])]
    copies[0].start()
    for u in range(8):
        at = slice(u * ROWS, (u + 1) * ROWS)
        wg_v[at] = wg_ref[u].astype(F32)
        copies.append(pltpu.make_async_copy(wg_v.at[at], wg_o.at[at], sem.at[u]))
        copies[-1].start()
    for i, (src, mid, dst) in enumerate(((dk_ref, dk_v, dk_o), (dv_ref, dv_v, dv_o))):
        mid[...] = (src[0].astype(F32) + src[1].astype(F32)).astype(BF16)
        copies.append(pltpu.make_async_copy(mid, dst, sem.at[9 + i]))
        copies[-1].start()
    for copy in copies:
        copy.wait()


def per_device(queries, keys, values, out_grad, out_weight, slopes, counts, gaps):
    width = queries.shape[2]
    nz = lax.axis_size("tensor")
    vmem, hbm = pl.BlockSpec(memory_space=pltpu.VMEM), pl.BlockSpec(memory_space=pltpu.HBM)

    def v(dtype, *shape):
        return pltpu.VMEM(shape, dtype)

    dq, dk, dv, wg = pl.pallas_call(
        kernel,
        out_shape=(
            v(BF16, ROWS, width),
            v(BF16, 2, ROWS, width),
            v(BF16, 2, ROWS, width),
            v(BF16, 8, ROWS, width),
        ),
        in_specs=[vmem, vmem, vmem, hbm, hbm, hbm, hbm, hbm],
        out_specs=(vmem, vmem, vmem, vmem),
        scratch_shapes=[
            v(F32, 8, ROWS),
            v(F32, 8, 8, ROWS),
            v(BF16, 8 * ROWS, ROWS),
            v(BF16, 8 * ROWS, ROWS),
            v(BF16, 4, ROWS, ROWS),
            v(BF16, 4, ROWS, ROWS),
            v(BF16, nz, ROWS, width),
            v(BF16, 4, ROWS, width),
            v(BF16, 2, *out_weight.shape),
            v(F32, 4, ROWS, 8 * ROWS),
            v(BF16, 4, ROWS, ROWS),
            v(BF16, ROWS, width),
            v(BF16, ROWS, width),
            v(BF16, ROWS, width),
            v(F32, ROWS, width),
            v(F32, ROWS, width),
            v(F32, ROWS, width),
            v(BF16, ROWS, width),
            v(BF16, 4, ROWS, ROWS),
            v(F32, 8 * ROWS, ROWS),
            v(F32, 8 * ROWS, ROWS),
            v(BF16, 8 * ROWS, ROWS),
            v(BF16, 8 * ROWS, ROWS),
            v(F32, 2, 4, 4 * ROWS, HALF),
            v(BF16, 2, 4, 4 * ROWS, HALF),
            v(BF16, 2, 2, 2 * ROWS, HALF),
            v(BF16, 2, 2, 4 * ROWS, HALF),
            v(F32, 2, 4, ROWS, HALF),
            v(BF16, 2, 4, ROWS, HALF),
            v(BF16, 2, 2, ROWS // 2, HALF),
            v(BF16, 2, 2, ROWS, HALF),
            pltpu.SemaphoreType.DMA((95,)),
        ],
        compiler_params=pltpu.CompilerParams(
            collective_id=0, has_side_effects=True, vmem_limit_bytes=62 << 20
        ),
        name="block_backward",
    )(
        slopes.reshape(1, -1), counts, gaps,
        queries[0], keys[0], values[0], out_grad[0], out_weight,
    )
    dq, dk, dv, wg = pl.pallas_call(
        write_out,
        out_shape=(
            jax.ShapeDtypeStruct((ROWS, width), BF16),
            jax.ShapeDtypeStruct((ROWS, width), BF16),
            jax.ShapeDtypeStruct((ROWS, width), BF16),
            jax.ShapeDtypeStruct((8 * ROWS, width), F32),
        ),
        in_specs=[vmem] * 4,
        out_specs=(hbm,) * 4,
        scratch_shapes=[
            v(BF16, ROWS, width),
            v(BF16, ROWS, width),
            v(F32, 8 * ROWS, width),
            pltpu.SemaphoreType.DMA((11,)),
        ],
        compiler_params=pltpu.CompilerParams(vmem_limit_bytes=12 << 20),
        name="write_out",
    )(dq, dk, dv, wg)
    return dq[None], dk[None], dv[None], wg


def solution(mesh):
    rows = P("fsdp", "context", "tensor")
    weight = P("fsdp", "tensor")
    placed = (rows, rows, rows, rows, weight, P("tensor"), P("fsdp", "context"))
    return jax.shard_map(
        per_device,
        mesh=mesh,
        in_specs=placed + (P("fsdp", "context"),),
        out_specs=(rows, rows, rows, weight),
        check_vma=False,
    )
```

time: 79.6 us -> 73.8 us (0.927)
  the two profiles are of different devices: /device:TPU:4 before, /device:TPU:2 now
where the time goes in v3:
time: 73.8 us; the launch traced here: 73.3 us
  Pallas kernels  72 us (98%)
  between operations  1.29 us (2%)
    pallas_call x1, Pallas kernels, per_device(): pl.pallas_call(kernel, out_shape=(v(BF16, ROWS, width), v(BF16, 2, ROWS,...  70.5 us
    pallas_call x1, Pallas kernels, per_device(): pl.pallas_call(write_out, out_shape=(jax.ShapeDtypeStruct((ROWS, width),...  1.53 us

profile of v3, /device:TPU:2, one launch (start us, length us, event | category | flops | bytes accessed | tf_op | source)
XLA Modules:
  0.0 73.3 jit_solution(13169671109636134369)
XLA Ops:
  1.3 70.5 %block_backward.1 = (bf16[128,512]{1,0:T(8,128)(2,1)S(1)}, bf16[2,128,512]{2,1,0:T(8,128)(2,1)S(1)}, bf16[2,128,512]{2,1,0:T(8,128)(2,1)S(1)}, bf16[8,128,512]{2,1,0:T(8,128)(2,1)S(1)}) custom-call(f32[1,4]{1,0:T(1,128)} %bitcast.12, s32[1,1]{1,0:T(1,128)S(6)} %copy.12.counts_ref, s32[1,128]{1,0:T(1,128)} %gaps_ref.1, bf16[128,512]{1,0:T(8,128)(2,1)} %bitcast.8, ...), custom_call_target="tpu_custom_call" | custom-call | tf_op jit(solution)/shard_map/block_backward/pallas_call | solution.py:489
  71.8 1.5 %write_out.1 = (bf16[128,512]{1,0:T(8,128)(2,1)}, bf16[128,512]{1,0:T(8,128)(2,1)}, bf16[128,512]{1,0:T(8,128)(2,1)}, f32[1024,512]{1,0:T(8,128)}) custom-call(bf16[128,512]{1,0:T(8,128)(2,1)S(1)} %get-tuple-element.12.dq_ref, bf16[2,128,512]{2,1,0:T(8,128)(2,1)S(1)} %get-tuple-element.13.dk_ref, bf16[2,128,512]{2,1,0:T(8,128)(2,1)S(1)} %get-tuple-element.14.dv_ref, ...), custom_call_target="tpu_custom_call" | custom-call | tf_op jit(solution)/shard_map/write_out/pallas_call | solution.py:541

commit v4 on v3

--- a/solution.py
+++ b/solution.py
@@ -12,6 +12,8 @@
 NEG = -1e30
 ROWS = 128
 HALF = 256
+AXES = (0, 1, 0, 1)
+PAIRS = ((0, 1), (2, 3))
 
 
 def mm(a, b, ca, cb):
@@ -23,8 +25,8 @@
     dq_ref, dk_ref, dv_ref, wg_ref,
     gap_out, gap_all, k_all, v_all, q_head, g_head, g_all, g_far, w_all,
     prob, o_head, o_own, o_masked, o_far, hp_own, hp_out, hp_far, hg_out,
-    dq_out, dk_acc, dv_acc, dk_out, dv_out,
-    part, part_out, half_in, full_in, part2, part2_out, half2_in, full2_in,
+    dq_out, dk_acc, dv_acc, dkv_out, dkv_in, dkv_sum,
+    part, part_out, half_in, full_in, part2, part2_out, full2_in,
     sem,
 ):
     c, z, f = lax.axis_index("context"), lax.axis_index("tensor"), lax.axis_index("fsdp")
@@ -103,6 +105,7 @@
 
     barrier = pltpu.get_barrier_semaphore()
     greeted = [dev(c_=lax.rem(c + d, 8)) for d in range(1, 8)] + [right, left, partner, across]
+    greeted.append(dev(f_=(1 - xh) * 2 + core))
     for where in greeted:
         pl.semaphore_signal(barrier, inc=1, device_id=where, device_id_type=MESH)
     pl.semaphore_wait(barrier, len(greeted))
@@ -247,10 +250,10 @@
     ring(5)
     forward(0)
     forward(1)
-    ring(6)
-    w_pass(2)
     forward(2)
     forward(3)
+    w_pass(2)
+    ring(6)
     own_g.wait()
 
     at_of, at_hp, by_of, by_hp = (slots(1) for _ in range(4))
@@ -306,6 +309,54 @@
                 arrived(self.full.at[way, self.low], self.at + 2 + 2 * way)
                 arrived(self.full.at[way, self.high], self.at + 3 + 2 * way)
             return self.terms[self.own] + self.full[0].astype(F32) + self.full[1].astype(F32)
+
+    arrived(o_far, at_of)
+    outputs = jnp.concatenate([o_masked[...], o_far[...]], axis=0)
+    for j in range(4):
+        product = mm(both(j), outputs, 0, 0)
+        for n, axis in enumerate(AXES):
+            chunk = product[:, n * ROWS : (n + 1) * ROWS]
+            if axis == 0:
+                part[n, j] = chunk
+            else:
+                for i in range(4):
+                    part[n, i, j * ROWS : (j + 1) * ROWS] = chunk[i * ROWS : (i + 1) * ROWS]
+
+    class Exchange:
+        def __init__(self, axis, terms, out, full, by):
+            self.axis, self.terms, self.out, self.full = axis, terms, out, full
+            self.at, self.by, self.own = slots(1), by, place[axis]
+
+        def start(self):
+            for d in (2, 1, 3):
+                group = lax.rem(self.own + d, 4)
+                self.out[group] = self.terms[group].astype(BF16)
+                where = beside(self.axis, d)
+                send(self.out.at[group], self.full.at[d - 1], self.at, where, self.by)
+
+        def finish(self):
+            arrived(self.full, self.at)
+            return self.terms[self.own] + sum(self.full[d].astype(F32) for d in range(3))
+
+    by_first, by_second = slots(4), slots(1)
+    for n in range(4):
+        at_end(by_first + n, part_out.at[n, 0:3])
+    at_end(by_second, part2_out.at[:, 0:3])
+    first, second = [], []
+    for n, axis in enumerate(AXES):
+        bufs = (part.at[n], part_out.at[n], half_in.at[n], full_in.at[n])
+        first.append(Scatter(axis, *bufs, by_first + n))
+        bufs = (part2.at[n], part2_out.at[n], full2_in.at[n])
+        second.append(Exchange(1 - axis, *bufs, by_second))
+
+    def each(chunks, *calls):
+        for call in calls:
+            for n in chunks:
+                call(n)
+
+    one, two = PAIRS
+    each(one, lambda n: first[n].start())
+    each(one, lambda n: first[n].more())
 
     own_w.wait()
     for i in range(3):
@@ -322,25 +373,6 @@
     send(hp_out, hp_far, at_hp, partner, by_hp)
     at_end(by_hp, hp_out)
 
-    arrived(o_far, at_of)
-    outputs = jnp.concatenate([o_masked[...], o_far[...]], axis=0)
-    for j in range(4):
-        product = mm(both(j), outputs, 0, 0)
-        part[0, j] = product[:, 0:HALF]
-        for i in range(4):
-            part[1, i, j * ROWS : (j + 1) * ROWS] = product[i * ROWS : (i + 1) * ROWS, HALF:]
-
-    by_first, by_second = slots(2), slots(1)
-    for i in range(2):
-        at_end(by_first + i, part_out.at[i, 0:3])
-    at_end(by_second, part2_out.at[:, 0:3])
-    first = [
-        Scatter(i, part.at[i], part_out.at[i], half_in.at[i], full_in.at[i], by_first + i)
-        for i in range(2)
-    ]
-    for scatter in first:
-        scatter.start()
-
     arrived(hp_far, at_hp)
     hg_out[...] = jnp.where(live, hp_own[...] + hp_far[...], 0.0).astype(BF16)
     at_g, by_g = slots(1), slots(1)
@@ -350,15 +382,23 @@
         peer = head * 2 + side
         give(peer == c, cols(hg_out, head), g_head.at[y], at_g, dev(c_=peer), by_g)
 
-    for scatter in first:
-        scatter.more()
-    for scatter in first:
-        scatter.middle()
+    each(two, lambda n: first[n].start())
+    each(one, lambda n: first[n].middle())
+    each(two, lambda n: first[n].more())
+
+    def halfway(n):
+        part2[n] = first[n].finish().reshape(part2.shape[1:])
+        second[n].start()
+
+    each(two, lambda n: first[n].middle())
+    each(one, halfway)
 
     held = []
-    at_dq, at_dk, at_dv, by_dq, by_dkv = (slots(1) for _ in range(5))
+    at_dq, at_dk, at_dv, at_swap, by_dq, by_dk, by_dv, by_swap = (slots(1) for _ in range(8))
     at_end_heads(by_dq)
-    at_end(by_dkv, w_all.at[0, 0:448])
+    at_end(by_dk, o_head.at[0:3])
+    at_end(by_dv, o_head.at[0:3])
+    at_end(by_swap, dkv_in)
     arrived(g_head, at_g)
     for t in (3, 2, 1, 0):
         n = 2 * ROWS * (t + 1)
@@ -379,39 +419,41 @@
             dv_acc[0:n] += dv_part
         for s in (2 * t + 1, 2 * t):
             at = slice(s * ROWS, (s + 1) * ROWS)
-            dk_out[at] = (dk_acc[at] * scaling).astype(BF16)
-            dv_out[at] = dv_acc[at].astype(BF16)
+            dkv_out[s % 2, 0, t] = (dk_acc[at] * scaling).astype(BF16)
+            dkv_out[s % 2, 1, t] = dv_acc[at].astype(BF16)
 
     for d in range(4):
         t = lax.rem(y + d, 4)
         held.append((2 * t + lax.rem(xl + t, 2), dq_out.at[t], cols(dq_ref, y), at_dq, by_dq))
-    for d in range(8):
-        s = lax.rem(c + d, 8)
-        held.append((s, rows(dk_out, s), cols(dk_ref.at[xl], y), at_dk, by_dkv))
-        held.append((s, rows(dv_out, s), cols(dv_ref.at[xl], y), at_dv, by_dkv))
-
     def release(n):
         for _ in range(min(n, len(held))):
             peer, src, dst, index, by = held.pop(0)
             give(peer == c, src, dst, index, dev(c_=peer), by)
 
-    release(6)
-    second = [
-        Scatter(1 - i, part2.at[i], part2_out.at[i], half2_in.at[i], full2_in.at[i], by_second)
-        for i in range(2)
-    ]
-    for i in range(2):
-        part2[i] = first[i].finish().reshape(part2.shape[1:])
-        second[i].start()
-        second[i].more()
-    release(5)
-    for i in range(2):
-        second[i].middle()
-    release(4)
+    other = dev(c_=y * 2 + 1 - xl)
+
+    def swap(i):
+        src = dkv_out.at[1 - xl, i // 2, 2 * (i % 2) : 2 * (i % 2) + 2]
+        dst = dkv_in.at[i // 2, 2 * (i % 2) : 2 * (i % 2) + 2]
+        send(src, dst, at_swap, other, by_swap)
+
+
+    def add_swapped():
+        arrived(dkv_in, at_swap)
+        for t in range(4):
+            at = pl.ds(pl.multiple_of((2 * t + xl) * ROWS, ROWS), ROWS)
+            dkv_sum[0, t] = (dk_acc[at] * scaling + dkv_in[0, t].astype(F32)).astype(BF16)
+            dkv_sum[1, t] = (dv_acc[at] + dkv_in[1, t].astype(F32)).astype(BF16)
+        for d in range(4):
+            t = lax.rem(y + d, 4)
+            there = 2 * t + xl
+            held.append((there, dkv_sum.at[0, t], cols(dk_ref, y), at_dk, by_dk))
+            held.append((there, dkv_sum.at[1, t], cols(dv_ref, y), at_dv, by_dv))
+
+
     at_x, at_y, by_all = slots(2), slots(16), slots(1)
     at_end(by_all, wg_ref.at[0:7])
     near, back = beside(1, 1), beside(1, -1)
-    other = dev(c_=y * 2 + 1 - xl)
     below, above, far = (lax.rem(y + d, 4) for d in (3, 1, 2))
     columns = (xl * 4, (1 - xl) * 4)
     mid = ROWS // 2
@@ -419,36 +461,67 @@
     def unit(column, place_y, i):
         return wg_ref.at[column + place_y, :, i * HALF : (i + 1) * HALF]
 
-    for i in range(2):
+    def gather(i):
         mine = unit(columns[0], y, i)
-        mine[...] = second[i].finish().astype(BF16)
+        for n in PAIRS[i]:
+            at = slice(n * ROWS, (n + 1) * ROWS)
+            wg_ref[columns[0] + y, :, at] = second[n].finish().astype(BF16)
         send(mine, mine, at_x + i, other, by_all)
         send(mine, mine, at_y + 2 * i, near, by_all)
         send(mine, mine, at_y + 2 * i + 1, back, by_all)
-    release(3)
-    for i in range(2):
+
+    def pass_x(i):
         mine = unit(columns[1], y, i)
         arrived(mine, at_x + i)
         send(mine, mine, at_y + 4 + 2 * i, near, by_all)
         send(mine, mine, at_y + 4 + 2 * i + 1, back, by_all)
+
+    def pass_y(j, i):
+        low = unit(columns[j], below, i)
+        arrived(low, at_y + 4 * j + 2 * i)
+        send(low.at[0:mid], low.at[0:mid], at_y + 8 + 4 * j + 2 * i, near, by_all)
+        high = unit(columns[j], above, i)
+        arrived(high, at_y + 4 * j + 2 * i + 1)
+        send(high.at[mid:], high.at[mid:], at_y + 9 + 4 * j + 2 * i, back, by_all)
+
+    def pass_x_last():
+        low = unit(columns[0], below, 1)
+        arrived(low, at_y + 2)
+        send(low.at[0:mid], low.at[0:mid], at_y + 10, near, by_all)
+        send(low, low, at_y + 6, other, by_all)
+        high = unit(columns[0], above, 1)
+        arrived(high, at_y + 3)
+        send(high.at[mid:], high.at[mid:], at_y + 11, back, by_all)
+        send(high, high, at_y + 7, other, by_all)
+
+    release(2)
+    swap(0)
+    each(two, halfway)
+    release(2)
+    gather(0)
+    swap(1)
+    gather(1)
+    swap(2)
+    pass_x(0)
+    swap(3)
+    pass_y(0, 0)
+    pass_x_last()
+    pass_y(1, 0)
+    add_swapped()
     release(len(held))
-    for j, column in enumerate(columns):
-        for i in range(2):
-            low = unit(column, below, i)
-            arrived(low, at_y + 4 * j + 2 * i)
-            send(low.at[0:mid], low.at[0:mid], at_y + 8 + 4 * j + 2 * i, near, by_all)
-            high = unit(column, above, i)
-            arrived(high, at_y + 4 * j + 2 * i + 1)
-            send(high.at[mid:], high.at[mid:], at_y + 9 + 4 * j + 2 * i, back, by_all)
-
+    end = unit(columns[0], far, 1)
+    arrived(end.at[0:mid], at_y + 10)
+    arrived(end.at[mid:], at_y + 11)
+    send(end, end, at_y + 14, other, by_all)
     arrived(dq_ref, at_dq)
     arrived(dk_ref, at_dk)
     arrived(dv_ref, at_dv)
     for j, column in enumerate(columns):
-        for i in range(2):
-            end = unit(column, far, i)
-            arrived(end.at[0:mid], at_y + 8 + 4 * j + 2 * i)
-            arrived(end.at[mid:], at_y + 9 + 4 * j + 2 * i)
+        end = unit(column, far, 0)
+        arrived(end.at[0:mid], at_y + 8 + 4 * j)
+        arrived(end.at[mid:], at_y + 9 + 4 * j)
+    for place_y, index in ((y, at_x + 1), (below, at_y + 6), (above, at_y + 7), (far, at_y + 14)):
+        arrived(unit(columns[1], place_y, 1), index)
 
     for group, ref, when in finals:
         wait = pltpu.make_async_remote_copy(
@@ -459,20 +532,19 @@
             wait()
         else:
             pl.when(when)(wait)
-    assert next(semaphores) == sem.shape[0], next(semaphores)
-
-
-def write_out(dq_ref, dk_ref, dv_ref, wg_ref, dq_o, dk_o, dv_o, wg_o, dk_v, dv_v, wg_v, sem):
-    copies = [pltpu.make_async_copy(dq_ref, dq_o, sem.at[8])]
-    copies[0].start()
+    used = next(semaphores)
+    assert used == sem.shape[0], used
+
+
+def write_out(dq_ref, dk_ref, dv_ref, wg_ref, dq_o, dk_o, dv_o, wg_o, wg_v, sem):
+    copies = []
     for u in range(8):
         at = slice(u * ROWS, (u + 1) * ROWS)
         wg_v[at] = wg_ref[u].astype(F32)
         copies.append(pltpu.make_async_copy(wg_v.at[at], wg_o.at[at], sem.at[u]))
         copies[-1].start()
-    for i, (src, mid, dst) in enumerate(((dk_ref, dk_v, dk_o), (dv_ref, dv_v, dv_o))):
-        mid[...] = (src[0].astype(F32) + src[1].astype(F32)).astype(BF16)
-        copies.append(pltpu.make_async_copy(mid, dst, sem.at[9 + i]))
+    for i, (src, dst) in enumerate(((dq_ref, dq_o), (dk_ref, dk_o), (dv_ref, dv_o))):
+        copies.append(pltpu.make_async_copy(src, dst, sem.at[8 + i]))
         copies[-1].start()
     for copy in copies:
         copy.wait()
@@ -490,8 +562,8 @@
         kernel,
         out_shape=(
             v(BF16, ROWS, width),
-            v(BF16, 2, ROWS, width),
-            v(BF16, 2, ROWS, width),
+            v(BF16, ROWS, width),
+            v(BF16, ROWS, width),
             v(BF16, 8, ROWS, width),
         ),
         in_specs=[vmem, vmem, vmem, hbm, hbm, hbm, hbm, hbm],
@@ -518,17 +590,17 @@
             v(BF16, 4, ROWS, ROWS),
             v(F32, 8 * ROWS, ROWS),
             v(F32, 8 * ROWS, ROWS),
-            v(BF16, 8 * ROWS, ROWS),
-            v(BF16, 8 * ROWS, ROWS),
-            v(F32, 2, 4, 4 * ROWS, HALF),
-            v(BF16, 2, 4, 4 * ROWS, HALF),
-            v(BF16, 2, 2, 2 * ROWS, HALF),
-            v(BF16, 2, 2, 4 * ROWS, HALF),
-            v(F32, 2, 4, ROWS, HALF),
-            v(BF16, 2, 4, ROWS, HALF),
-            v(BF16, 2, 2, ROWS // 2, HALF),
-            v(BF16, 2, 2, ROWS, HALF),
-            pltpu.SemaphoreType.DMA((95,)),
+            v(BF16, 2, 2, 4, ROWS, ROWS),
+            v(BF16, 2, 4, ROWS, ROWS),
+            v(BF16, 2, 4, ROWS, ROWS),
+            v(F32, 4, 4, 4 * ROWS, ROWS),
+            v(BF16, 4, 4, 4 * ROWS, ROWS),
+            v(BF16, 4, 2, 2 * ROWS, ROWS),
+            v(BF16, 4, 2, 4 * ROWS, ROWS),
+            v(F32, 4, 4, ROWS, ROWS),
+            v(BF16, 4, 4, ROWS, ROWS),
+            v(BF16, 4, 3, ROWS, ROWS),
+            pltpu.SemaphoreType.DMA((104,)),
         ],
         compiler_params=pltpu.CompilerParams(
             collective_id=0, has_side_effects=True, vmem_limit_bytes=62 << 20
@@ -549,8 +621,6 @@
         in_specs=[vmem] * 4,
         out_specs=(hbm,) * 4,
         scratch_shapes=[
-            v(BF16, ROWS, width),
-            v(BF16, ROWS, width),
             v(F32, 8 * ROWS, width),
             pltpu.SemaphoreType.DMA((11,)),
         ],

time: 73.8 us -> 64.8 us (0.88)
  Pallas kernels: 72 us -> 63.4 us
    pallas_call x1, Pallas kernels: 70.5 us -> 61.9 us  [per_device(): pl.pallas_call(kernel, out_shape=(v(BF16, ROWS, width), v(BF16, ROWS, wid...]
where the time goes in v4:
time: 64.8 us; the launch traced here: 64.7 us
  Pallas kernels  63.4 us (98%)
  between operations  1.29 us (2%)
    pallas_call x1, Pallas kernels, per_device(): pl.pallas_call(kernel, out_shape=(v(BF16, ROWS, width), v(BF16, ROWS, wid...  61.9 us
    pallas_call x1, Pallas kernels, per_device(): pl.pallas_call(write_out, out_shape=(jax.ShapeDtypeStruct((ROWS, width),...  1.54 us

profile of v4, /device:TPU:2, one launch (start us, length us, event | category | flops | bytes accessed | tf_op | source)
XLA Modules:
  0.0 64.7 jit_solution(10330206985547380215)
XLA Ops:
  1.3 61.9 %block_backward.1 = (bf16[128,512]{1,0:T(8,128)(2,1)S(1)}, bf16[128,512]{1,0:T(8,128)(2,1)S(1)}, bf16[128,512]{1,0:T(8,128)(2,1)S(1)}, bf16[8,128,512]{2,1,0:T(8,128)(2,1)S(1)}) custom-call(f32[1,4]{1,0:T(1,128)} %bitcast.12, s32[1,1]{1,0:T(1,128)S(6)} %copy.12.counts_ref, s32[1,128]{1,0:T(1,128)} %gaps_ref.1, bf16[128,512]{1,0:T(8,128)(2,1)} %bitcast.8, ...), custom_call_target="tpu_custom_call" | custom-call | tf_op jit(solution)/shard_map/block_backward/pallas_call | solution.py:561
  63.2 1.5 %write_out.1 = (bf16[128,512]{1,0:T(8,128)(2,1)}, bf16[128,512]{1,0:T(8,128)(2,1)}, bf16[128,512]{1,0:T(8,128)(2,1)}, f32[1024,512]{1,0:T(8,128)}) custom-call(bf16[128,512]{1,0:T(8,128)(2,1)S(1)} %get-tuple-element.12.dq_ref, bf16[128,512]{1,0:T(8,128)(2,1)S(1)} %get-tuple-element.13.dk_ref, bf16[128,512]{1,0:T(8,128)(2,1)S(1)} %get-tuple-element.14.dv_ref, ...), custom_call_target="tpu_custom_call" | custom-call | tf_op jit(solution)/shard_map/write_out/pallas_call | solution.py:613

commit v5 on v4

--- a/solution.py
+++ b/solution.py
@@ -246,12 +246,12 @@
     ring(2)
     ring(3)
     ring(4)
-    w_pass(1)
-    ring(5)
     forward(0)
     forward(1)
+    ring(5)
     forward(2)
     forward(3)
+    w_pass(1)
     w_pass(2)
     ring(6)
     own_g.wait()
@@ -390,11 +390,9 @@
         part2[n] = first[n].finish().reshape(part2.shape[1:])
         second[n].start()
 
-    each(two, lambda n: first[n].middle())
-    each(one, halfway)
-
     held = []
-    at_dq, at_dk, at_dv, at_swap, by_dq, by_dk, by_dv, by_swap = (slots(1) for _ in range(8))
+    at_dq, at_dk, at_dv, by_dq, by_dk, by_dv, by_swap = (slots(1) for _ in range(7))
+    at_swap = slots(2)
     at_end_heads(by_dq)
     at_end(by_dk, o_head.at[0:3])
     at_end(by_dv, o_head.at[0:3])
@@ -435,20 +433,19 @@
     def swap(i):
         src = dkv_out.at[1 - xl, i // 2, 2 * (i % 2) : 2 * (i % 2) + 2]
         dst = dkv_in.at[i // 2, 2 * (i % 2) : 2 * (i % 2) + 2]
-        send(src, dst, at_swap, other, by_swap)
-
-
-    def add_swapped():
-        arrived(dkv_in, at_swap)
+        send(src, dst, at_swap + i // 2, other, by_swap)
+
+
+    def add_swapped(i):
+        arrived(dkv_in.at[i], at_swap + i)
         for t in range(4):
             at = pl.ds(pl.multiple_of((2 * t + xl) * ROWS, ROWS), ROWS)
-            dkv_sum[0, t] = (dk_acc[at] * scaling + dkv_in[0, t].astype(F32)).astype(BF16)
-            dkv_sum[1, t] = (dv_acc[at] + dkv_in[1, t].astype(F32)).astype(BF16)
+            mine = dk_acc[at] * scaling if i == 0 else dv_acc[at]
+            dkv_sum[i, t] = (mine + dkv_in[i, t].astype(F32)).astype(BF16)
+        dst, index, by = ((dk_ref, at_dk, by_dk), (dv_ref, at_dv, by_dv))[i]
         for d in range(4):
             t = lax.rem(y + d, 4)
-            there = 2 * t + xl
-            held.append((there, dkv_sum.at[0, t], cols(dk_ref, y), at_dk, by_dk))
-            held.append((there, dkv_sum.at[1, t], cols(dv_ref, y), at_dv, by_dv))
+            held.append((2 * t + xl, dkv_sum.at[i, t], cols(dst, y), index, by))
 
 
     at_x, at_y, by_all = slots(2), slots(16), slots(1)
@@ -494,21 +491,25 @@
         send(high.at[mid:], high.at[mid:], at_y + 11, back, by_all)
         send(high, high, at_y + 7, other, by_all)
 
-    release(2)
+    each(two, lambda n: first[n].middle())
+    each(one, halfway)
     swap(0)
     each(two, halfway)
-    release(2)
     gather(0)
     swap(1)
+    release(2)
     gather(1)
     swap(2)
+    release(2)
     pass_x(0)
     swap(3)
+    add_swapped(0)
+    release(4)
     pass_y(0, 0)
     pass_x_last()
     pass_y(1, 0)
-    add_swapped()
-    release(len(held))
+    add_swapped(1)
+    release(4)
     end = unit(columns[0], far, 1)
     arrived(end.at[0:mid], at_y + 10)
     arrived(end.at[mid:], at_y + 11)
@@ -600,7 +601,7 @@
             v(F32, 4, 4, ROWS, ROWS),
             v(BF16, 4, 4, ROWS, ROWS),
             v(BF16, 4, 3, ROWS, ROWS),
-            pltpu.SemaphoreType.DMA((104,)),
+            pltpu.SemaphoreType.DMA((105,)),
         ],
         compiler_params=pltpu.CompilerParams(
             collective_id=0, has_side_effects=True, vmem_limit_bytes=62 << 20

time: 64.8 us -> 63.9 us (0.986)
  Pallas kernels: 63.4 us -> 62.5 us
    pallas_call x1, Pallas kernels: 61.9 us -> 60.9 us  [per_device(): pl.pallas_call(kernel, out_shape=(v(BF16, ROWS, width), v(BF16, ROWS, wid...]
where the time goes in v5:
time: 63.9 us; the launch traced here: 63.8 us
  Pallas kernels  62.5 us (98%)
  between operations  1.29 us (2%)
    pallas_call x1, Pallas kernels, per_device(): pl.pallas_call(kernel, out_shape=(v(BF16, ROWS, width), v(BF16, ROWS, wid...  60.9 us
    pallas_call x1, Pallas kernels, per_device(): pl.pallas_call(write_out, out_shape=(jax.ShapeDtypeStruct((ROWS, width),...  1.54 us

profile of v5, /device:TPU:2, one launch (start us, length us, event | category | flops | bytes accessed | tf_op | source)
XLA Modules:
  0.0 63.8 jit_solution(5483562372598817628)
XLA Ops:
  1.3 60.9 %block_backward.1 = (bf16[128,512]{1,0:T(8,128)(2,1)S(1)}, bf16[128,512]{1,0:T(8,128)(2,1)S(1)}, bf16[128,512]{1,0:T(8,128)(2,1)S(1)}, bf16[8,128,512]{2,1,0:T(8,128)(2,1)S(1)}) custom-call(f32[1,4]{1,0:T(1,128)} %bitcast.12, s32[1,1]{1,0:T(1,128)S(6)} %copy.12.counts_ref, s32[1,128]{1,0:T(1,128)} %gaps_ref.1, bf16[128,512]{1,0:T(8,128)(2,1)} %bitcast.8, ...), custom_call_target="tpu_custom_call" | custom-call | tf_op jit(solution)/shard_map/block_backward/pallas_call | solution.py:562
  62.2 1.5 %write_out.1 = (bf16[128,512]{1,0:T(8,128)(2,1)}, bf16[128,512]{1,0:T(8,128)(2,1)}, bf16[128,512]{1,0:T(8,128)(2,1)}, f32[1024,512]{1,0:T(8,128)}) custom-call(bf16[128,512]{1,0:T(8,128)(2,1)S(1)} %get-tuple-element.12.dq_ref, bf16[128,512]{1,0:T(8,128)(2,1)S(1)} %get-tuple-element.13.dk_ref, bf16[128,512]{1,0:T(8,128)(2,1)S(1)} %get-tuple-element.14.dv_ref, ...), custom_call_target="tpu_custom_call" | custom-call | tf_op jit(solution)/shard_map/write_out/pallas_call | solution.py:614

commit v6 on v5

--- a/solution.py
+++ b/solution.py
@@ -95,6 +95,11 @@
     def rows(ref, shard):
         return ref.at[pl.ds(pl.multiple_of(shard * ROWS, ROWS), ROWS)]
 
+    barrier = pltpu.get_barrier_semaphore()
+    greeted = [dev(c_=lax.rem(c + d, 8)) for d in range(1, 8)] + [right, left, partner, across]
+    greeted.append(dev(f_=(1 - xh) * 2 + core))
+    for where in greeted:
+        pl.semaphore_signal(barrier, inc=1, device_id=where, device_id_type=MESH)
     lane8 = lax.broadcasted_iota(jnp.int32, (8, ROWS), 1)
     row8 = lax.broadcasted_iota(jnp.int32, (8, ROWS), 0)
     gap_out[...] = jnp.where(
@@ -102,12 +107,6 @@
     ).astype(F32)
     heads = lax.broadcasted_iota(jnp.int32, slopes_ref.shape, 1)
     slope = jnp.sum(jnp.where(heads == y, slopes_ref[...], 0.0), axis=1, keepdims=True)
-
-    barrier = pltpu.get_barrier_semaphore()
-    greeted = [dev(c_=lax.rem(c + d, 8)) for d in range(1, 8)] + [right, left, partner, across]
-    greeted.append(dev(f_=(1 - xh) * 2 + core))
-    for where in greeted:
-        pl.semaphore_signal(barrier, inc=1, device_id=where, device_id_type=MESH)
     pl.semaphore_wait(barrier, len(greeted))
 
     at_gap, at_kvq, at_ring, at_far, at_w = slots(1), slots(4), slots(2 * nz), slots(1), slots(7)
@@ -539,13 +538,13 @@
 
 def write_out(dq_ref, dk_ref, dv_ref, wg_ref, dq_o, dk_o, dv_o, wg_o, wg_v, sem):
     copies = []
+    for i, (src, dst) in enumerate(((dq_ref, dq_o), (dk_ref, dk_o), (dv_ref, dv_o))):
+        copies.append(pltpu.make_async_copy(src, dst, sem.at[8 + i]))
+        copies[-1].start()
     for u in range(8):
         at = slice(u * ROWS, (u + 1) * ROWS)
         wg_v[at] = wg_ref[u].astype(F32)
         copies.append(pltpu.make_async_copy(wg_v.at[at], wg_o.at[at], sem.at[u]))
-        copies[-1].start()
-    for i, (src, dst) in enumerate(((dq_ref, dq_o), (dk_ref, dk_o), (dv_ref, dv_o))):
-        copies.append(pltpu.make_async_copy(src, dst, sem.at[8 + i]))
         copies[-1].start()
     for copy in copies:
         copy.wait()

time: 63.9 us -> 63.8 us (level)
  no operation moved by 1% of the time
where the time goes in v6:
time: 63.8 us; the launch traced here: 63.7 us
  Pallas kernels  62.4 us (98%)
  between operations  1.29 us (2%)
    pallas_call x1, Pallas kernels, per_device(): pl.pallas_call(kernel, out_shape=(v(BF16, ROWS, width), v(BF16, ROWS, wid...  60.9 us
    pallas_call x1, Pallas kernels, per_device(): pl.pallas_call(write_out, out_shape=(jax.ShapeDtypeStruct((ROWS, width),...  1.53 us

profile of v6, /device:TPU:2, one launch (start us, length us, event | category | flops | bytes accessed | tf_op | source)
XLA Modules:
  0.0 63.7 jit_solution(5839840990180754385)
XLA Ops:
  1.3 60.9 %block_backward.1 = (bf16[128,512]{1,0:T(8,128)(2,1)S(1)}, bf16[128,512]{1,0:T(8,128)(2,1)S(1)}, bf16[128,512]{1,0:T(8,128)(2,1)S(1)}, bf16[8,128,512]{2,1,0:T(8,128)(2,1)S(1)}) custom-call(f32[1,4]{1,0:T(1,128)} %bitcast.12, s32[1,1]{1,0:T(1,128)S(6)} %copy.12.counts_ref, s32[1,128]{1,0:T(1,128)} %gaps_ref.1, bf16[128,512]{1,0:T(8,128)(2,1)} %bitcast.8, ...), custom_call_target="tpu_custom_call" | custom-call | tf_op jit(solution)/shard_map/block_backward/pallas_call | solution.py:561
  62.1 1.5 %write_out.1 = (bf16[128,512]{1,0:T(8,128)(2,1)}, bf16[128,512]{1,0:T(8,128)(2,1)}, bf16[128,512]{1,0:T(8,128)(2,1)}, f32[1024,512]{1,0:T(8,128)}) custom-call(bf16[128,512]{1,0:T(8,128)(2,1)S(1)} %get-tuple-element.12.dq_ref, bf16[128,512]{1,0:T(8,128)(2,1)S(1)} %get-tuple-element.13.dk_ref, bf16[128,512]{1,0:T(8,128)(2,1)S(1)} %get-tuple-element.14.dv_ref, ...), custom_call_target="tpu_custom_call" | custom-call | tf_op jit(solution)/shard_map/write_out/pallas_call | solution.py:613
